TPU v7x, 256 devices: a whole 4x4x8 slice. The times are simulated.
256 devices in a mesh: dp: 8 (over z_lo, x), ctx: 32 (over y, z_hi, core).
Axes of the slice: x: 4, y: 4, z: 8 (z_hi: 4, z_lo: 2; z = z_hi * 2 + z_lo), core: 2. Of those that a mesh axis runs over, the one named last changes fastest.
Arguments:
- grad_out: bfloat16 [8, 4096, 2048], P('dp', 'ctx'), may hold values from -6 to 6
- saved_input: bfloat16 [8, 4096, 2048], P('dp', 'ctx'), may hold values from -6 to 6
- gate_value: bfloat16 [8, 4096, 2048], P('dp', 'ctx'), may hold values from -6 to 6
- filter_taps: bfloat16 [2048, 4096], P(None, 'ctx'), may hold values from -0.09375 to 0.09375
- skip_gain: float32 [2048], replicated, may hold values from 0.1 to 1.9
- lang_ids: int32 [8, 4096], P('dp', 'ctx'), may hold values from 0 to 15
- doc_ids: int32 [8, 4096], P('dp', 'ctx'), may hold values from 0 to 31, never falling along the last dimension, each value on 1 to 1024 neighbouring positions
- dro_weight: float32 [16], replicated, may hold values from 0.25 to 4
Outputs:
- d_input: bfloat16 [8, 4096, 2048], P('dp', 'ctx')
- d_gate: bfloat16 [8, 4096, 2048], P('dp', 'ctx')
- d_filter: float32 [2048, 4096], P('ctx', 'dp')
Inputs may be any that keep to these rules, and one draw needn't show every extreme that they name: `doc_ids`: in each sequence the document numbers never fall, and every number from 0 to 31 occurs.
All inputs are finite; a program needn't handle non-finite values.
Results may differ from a plain program's by a relative error of at most 0.017.
Values may be sent and summed in bfloat16 or wider, within the bound.
A program may use at most 128 MiB of HBM per device.

v0:
```python
import math

import jax
import jax.numpy as jnp
from jax import lax
from jax.sharding import PartitionSpec as P

NDOCS = 32


highest = lax.Precision.HIGHEST


def angles(first, second, period):
    return 2.0 * math.pi / period * (first * second % period).astype(jnp.float32)


def spectral_tables(length):
    size = 2 * length
    rows = size // 128
    half = length // 128
    outer = angles(
        jnp.arange(half, dtype=jnp.int32)[:, None], jnp.arange(rows, dtype=jnp.int32)[None, :], rows
    )
    twist = angles(
        jnp.arange(rows, dtype=jnp.int32)[:, None], jnp.arange(128, dtype=jnp.int32)[None, :], size
    )
    inner = angles(
        jnp.arange(128, dtype=jnp.int32)[:, None], jnp.arange(128, dtype=jnp.int32)[None, :], 128
    )
    return (
        jnp.cos(outer),
        jnp.sin(outer),
        jnp.cos(twist),
        jnp.sin(twist),
        jnp.cos(inner),
        jnp.sin(inner),
    )


def forward(signal, tables):
    cos_out, sin_out, cos_tw, sin_tw, cos_in, sin_in = tables
    count = signal.shape[0]
    shaped = signal.reshape(count, cos_out.shape[0], 128)
    first_re = jnp.einsum("cpn,pk->ckn", shaped, cos_out, precision=highest)
    first_im = -jnp.einsum("cpn,pk->ckn", shaped, sin_out, precision=highest)
    turned_re = first_re * cos_tw + first_im * sin_tw
    turned_im = first_im * cos_tw - first_re * sin_tw
    spec_re = jnp.einsum("ckn,nm->ckm", turned_re, cos_in, precision=highest) + jnp.einsum(
        "ckn,nm->ckm", turned_im, sin_in, precision=highest
    )
    spec_im = jnp.einsum("ckn,nm->ckm", turned_im, cos_in, precision=highest) - jnp.einsum(
        "ckn,nm->ckm", turned_re, sin_in, precision=highest
    )
    return (spec_re, spec_im)


def inverse(spec_re, spec_im, tables):
    cos_out, sin_out, cos_tw, sin_tw, cos_in, sin_in = tables
    count = spec_re.shape[0]
    size = spec_re.shape[1] * 128
    part_re = jnp.einsum("ckm,mn->ckn", spec_re, cos_in, precision=highest) - jnp.einsum(
        "ckm,mn->ckn", spec_im, sin_in, precision=highest
    )
    part_im = jnp.einsum("ckm,mn->ckn", spec_im, cos_in, precision=highest) + jnp.einsum(
        "ckm,mn->ckn", spec_re, sin_in, precision=highest
    )
    turned_re = part_re * cos_tw - part_im * sin_tw
    turned_im = part_im * cos_tw + part_re * sin_tw
    signal = jnp.einsum("ckn,pk->cpn", turned_re, cos_out, precision=highest) - jnp.einsum(
        "ckn,pk->cpn", turned_im, sin_out, precision=highest
    )
    return signal.reshape(count, cos_out.shape[0] * 128) / size


def local(grad_out, saved_input, gate_value, filter_taps, skip_gain, lang_ids, doc_ids, dro_weight):
    tokens = grad_out.shape[1]
    channels = grad_out.shape[2]
    pieces = lax.axis_size("ctx")
    length = tokens * pieces
    span = channels // pieces
    lang_hot = lang_ids[0][:, None] == jnp.arange(dro_weight.shape[0], dtype=jnp.int32)[None, :]
    group_weight = jnp.sum(
        jnp.where(lang_hot, dro_weight[None, :], jnp.zeros_like(dro_weight)[None, :]), axis=1
    )
    doc_hot = (doc_ids[0][:, None] == jnp.arange(NDOCS, dtype=jnp.int32)[None, :]).astype(
        jnp.float32
    )
    counts = lax.psum(jnp.sum(doc_hot, axis=0), "ctx")
    doc_len = jnp.sum(doc_hot * counts[None, :], axis=1)
    mean_len = length / NDOCS
    scale = group_weight * (2.0 * mean_len) / (doc_len + mean_len)
    grad_scaled = grad_out[0].astype(jnp.float32) * scale[:, None]
    grad_conv = (grad_scaled * gate_value[0].astype(jnp.float32)).astype(jnp.bfloat16)
    tables = spectral_tables(length)
    skip_local = lax.dynamic_slice_in_dim(skip_gain, lax.axis_index("ctx") * span, span)[:, None]
    input_slab = saved_input[0].T
    grad_slab = grad_conv.T
    members = lax.axis_size("dp")
    share = span // members
    blocks = filter_taps.reshape(pieces, span, tokens)
    own_taps = lax.dynamic_slice_in_dim(blocks, lax.axis_index("dp") * share, share, 1).reshape(
        pieces * share, tokens
    )
    input_pen, grad_pen, filter_pen = (
        lax.all_to_all(input_slab, "ctx", split_axis=0, concat_axis=1, tiled=True),
        lax.all_to_all(grad_slab, "ctx", split_axis=0, concat_axis=1, tiled=True),
        lax.all_to_all(own_taps, "ctx", split_axis=0, concat_axis=1, tiled=True),
    )
    share_re, share_im = forward(filter_pen.astype(jnp.float32), tables)
    filt_re, filt_im = (
        lax.all_gather(share_re.astype(jnp.bfloat16), "dp", axis=0, tiled=True).astype(
            share_re.dtype
        ),
        lax.all_gather(share_im.astype(jnp.bfloat16), "dp", axis=0, tiled=True).astype(
            share_im.dtype
        ),
    )
    input_full = input_pen.astype(jnp.float32)
    grad_full = grad_pen.astype(jnp.float32)
    input_re, input_im = forward(input_full, tables)
    grad_re, grad_im = forward(grad_full, tables)
    mixed = inverse(
        filt_re * input_re - filt_im * input_im, filt_re * input_im + filt_im * input_re, tables
    )
    mixed_pen = (mixed + skip_local * input_full).astype(jnp.bfloat16)
    back = inverse(
        filt_re * grad_re + filt_im * grad_im, filt_re * grad_im - filt_im * grad_re, tables
    )
    mixed_slab = lax.all_to_all(mixed_pen, "ctx", split_axis=1, concat_axis=0, tiled=True)
    input_back = lax.all_to_all(
        (back + skip_local * grad_full).astype(jnp.bfloat16),
        "ctx",
        split_axis=1,
        concat_axis=0,
        tiled=True,
    )
    lagged = inverse(
        input_re * grad_re + input_im * grad_im, input_re * grad_im - input_im * grad_re, tables
    )
    filter_grad = lax.psum_scatter(
        lagged.astype(jnp.bfloat16), "dp", scatter_dimension=1, tiled=True
    ).astype(jnp.float32)
    d_gate = (grad_scaled * mixed_slab.T.astype(jnp.float32)).astype(jnp.bfloat16)
    return (input_back.T[None], d_gate[None], filter_grad)


def solution(mesh):
    return jax.shard_map(
        local,
        mesh=mesh,
        in_specs=(
            P("dp", "ctx", None),
            P("dp", "ctx", None),
            P("dp", "ctx", None),
            P(None, "ctx"),
            P(),
            P("dp", "ctx"),
            P("dp", "ctx"),
            P(),
        ),
        out_specs=(P("dp", "ctx", None), P("dp", "ctx", None), P("ctx", "dp")),
        check_vma=False,
    )
```

profile of v0, /device:TPU:1, one launch (start us, length us, event | category | flops | bytes accessed | tf_op | source)
XLA Modules:
  0.0 322.6 jit_solution(1731337726296936049)
XLA Ops:
  7.2 1.0 copy-done
  8.9 12.8 %all-to-all-start = ((bf16[32,8,128]{2,1,0:T(8,128)(2,1)}), bf16[32,8,128]{2,1,0:T(8,128)(2,1)S(1)}, u32[]{:S(2)}, u32[]{:S(2)}) async-start(bf16[32,8,128]{2,1,0:T(8,128)(2,1)} %constant_dynamic-slice_fusion), calls=%async_computation | async-start | bytes 131072 | tf_op jit(solution)/shard_map/all_to_all | solution.py:108
  21.8 9.7 %all-to-all-done = bf16[32,8,128]{2,1,0:T(8,128)(2,1)S(1)} async-done(((bf16[32,8,128]{2,1,0:T(8,128)(2,1)}), bf16[32,8,128]{2,1,0:T(8,128)(2,1)S(1)}, u32[]{:S(2)}, u32[]{:S(2)}) %all-to-all-start) | async-done | bytes 65568 | tf_op jit(solution)/shard_map/all_to_all | solution.py:108
  32.9 1.3 fusion.96
  35.2 3.9 %all-to-all-start.3 = ((bf16[32,64,128]{2,1,0:T(8,128)(2,1)}), bf16[32,64,128]{2,1,0:T(8,128)(2,1)S(1)}, u32[]{:S(2)}, u32[]{:S(2)}) async-start(bf16[32,64,128]{2,1,0:T(8,128)(2,1)} %bitcast.24), calls=%async_computation.3 | async-start | bytes 1048576 | tf_op jit(solution)/shard_map/all_to_all | solution.py:106
  40.8 1.3 fusion.95
  42.1 19.2 %all-to-all-done.3 = bf16[32,64,128]{2,1,0:T(8,128)(2,1)S(1)} async-done(((bf16[32,64,128]{2,1,0:T(8,128)(2,1)}), bf16[32,64,128]{2,1,0:T(8,128)(2,1)S(1)}, u32[]{:S(2)}, u32[]{:S(2)}) %all-to-all-start.3) | async-done | bytes 524320 | tf_op jit(solution)/shard_map/all_to_all | solution.py:106
  61.3 1.1 fusion.111
  62.4 1.1 fusion.113
  63.5 2.2 fusion.4
  65.7 2.2 fusion.6
  68.0 2.3 fusion.53
  70.3 3.9 %fusion.50 = f32[64,64,128]{2,1,0:T(8,128)} fusion(f32[64,64,128]{2,1,0:T(8,128)S(1)} %fusion.6, f32[64,64,128]{2,0,1:T(8,128)S(1)} %fusion.113, f32[64,64,128]{2,0,1:T(8,128)S(1)} %fusion.111, f32[64,128]{1,0:T(8,128)S(1)} %get-tuple-element.17, f32[64,128]{1,0:T(8,128)S(1)} %get-tuple-element.18), kind=kOutput, calls=%fused_computation.60 | convolution fusion | flops 808157184 | bytes 8454144 | tf_op jit(solution)/shard_map/ckn,nm->ckm/dot_general | solution.py:49
  74.2 39.1 %all-gather.3.cloned.1.call-done = bf16[64,64,128]{2,1,0:T(8,128)(2,1)} async-done(((bf16[8,64,128]{2,1,0:T(8,128)(2,1)}), bf16[64,64,128]{2,1,0:T(8,128)(2,1)}) %all-gather.3.cloned.1.call-update) | async-done | bytes 1048592 | tf_op jit(solution)/shard_map/all_gather | solution.py:112
  113.3 4.5 %fusion.148 = f32[64,64,128]{2,1,0:T(8,128)S(1)} fusion(f32[64,64,128]{2,1,0:T(8,128)S(1)} %fusion.53, bf16[64,64,128]{2,1,0:T(8,128)(2,1)} %all-gather.3.cloned.1.call-done, f32[64,64,128]{2,1,0:T(8,128)} %fusion.50, bf16[64,64,128]{2,1,0:T(8,128)(2,1)} %all-gather.5.cloned.1.call-done), kind=kOutput, calls=%fused_computation.146 | convolution fusion | flops 808157184 | bytes 8388608 | tf_op jit(solution)/shard_map/ckm,mn->ckn/dot_general | solution.py:65
  117.9 2.2 fusion.150
  120.2 2.3 convolution_add_fusion.1
  122.4 2.3 convolution_subtract_fusion.1
  124.7 1.4 fusion.28
  126.2 2.0 fusion.92
  129.2 14.5 %all-to-all-start.4 = ((bf16[64,32,128]{2,0,1:T(8,128)(2,1)}), bf16[64,32,128]{2,0,1:T(8,128)(2,1)S(1)}, u32[]{:S(2)}, u32[]{:S(2)}) async-start(bf16[64,32,128]{2,0,1:T(8,128)(2,1)} %copy.38), calls=%async_computation.4 | async-start | bytes 1048576 | tf_op jit(solution)/shard_map/all_to_all | solution.py:130
  143.7 1.3 copy.32
  145.1 2.0 copy.33
  147.2 72.4 %psum.7 = f32[32]{0:T(128)S(1)} all-reduce(f32[32]{0:T(128)S(1)} %convert_reduce_fusion), channel_id=1, replica_groups=mesh['dp'=8,'ctx'=32] {'ctx'}, use_global_device_ids=true, to_apply=%region_2.3 | all-reduce | flops 32 | bytes 256 | tf_op jit(solution)/shard_map/psum | solution.py:89
  219.8 2.1 fusion.97
  221.9 25.3 %all_to_all.71 = bf16[32,64,128]{2,1,0:T(8,128)(2,1)S(1)} all-to-all(bf16[32,64,128]{2,1,0:T(8,128)(2,1)S(1)} %bitcast.195), channel_id=1, replica_groups=mesh['dp'=8,'ctx'=32] {'ctx'}, dimensions={0} | all-to-all | bytes 1048576 | tf_op jit(solution)/shard_map/all_to_all | solution.py:107
  247.2 1.1 fusion.115
  248.4 1.1 fusion.117
  249.5 2.2 fusion.12
  251.7 2.2 fusion.14
  254.0 2.2 fusion.47
  256.2 4.1 %multiply_subtract_fusion = (f32[64,64,128]{2,1,0:T(8,128)S(1)}, f32[64,64,128]{2,1,0:T(8,128)S(1)}, f32[64,64,128]{2,1,0:T(8,128)}) fusion(f32[64,64,128]{2,1,0:T(8,128)S(1)} %fusion.53, f32[64,64,128]{2,1,0:T(8,128)S(1)} %copy-done.3, f32[64,64,128]{2,1,0:T(8,128)S(1)} %fusion.47, f32[64,64,128]{2,1,0:T(8,128)S(1)} %fusion.14, ...), kind=kOutput, calls=%fused_computation.36 | convolution fusion | flops 811302912 | bytes 18939904 | tf_op jit(solution)/shard_map/ckn,nm->ckm/dot_general | solution.py:49
  260.3 2.6 fusion.144
  262.9 2.1 fusion.146
  265.0 2.1 convolution_add_fusion
  267.1 2.1 convolution_subtract_fusion
  269.2 1.4 fusion.20
  270.7 1.5 fusion.86
  273.3 4.7 %fusion.154 = f32[64,64,128]{2,1,0:T(8,128)S(1)} fusion(f32[64,64,128]{2,1,0:T(8,128)S(1)} %copy-done.5, bf16[64,64,128]{2,1,0:T(8,128)(2,1)} %all-gather.3.cloned.1.call-done, f32[64,64,128]{2,1,0:T(8,128)} %get-tuple-element.16, bf16[64,64,128]{2,1,0:T(8,128)(2,1)} %all-gather.5.cloned.1.call-done), kind=kOutput, calls=%fused_computation.152 | convolution fusion | flops 808157184 | bytes 8388608 | tf_op jit(solution)/shard_map/ckm,mn->ckn/dot_general | solution.py:65
  278.0 2.2 fusion.156
  280.3 2.3 convolution_add_fusion.2
  282.6 2.3 convolution_subtract_fusion.2
  284.9 1.4 fusion.36
  286.3 1.8 fusion.89
  289.1 4.9 %all-to-all-start.2 = ((bf16[64,32,128]{2,0,1:T(8,128)(2,1)}), bf16[64,32,128]{2,0,1:T(8,128)(2,1)S(1)}, u32[]{:S(2)}, u32[]{:S(2)}) async-start(bf16[64,32,128]{2,0,1:T(8,128)(2,1)} %copy.35), calls=%async_computation.2 | async-start | bytes 1048576 | tf_op jit(solution)/shard_map/all_to_all | solution.py:131
  294.1 1.0 copy.40
  295.1 18.3 %all-to-all-done.2 = bf16[64,32,128]{2,0,1:T(8,128)(2,1)S(1)} async-done(((bf16[64,32,128]{2,0,1:T(8,128)(2,1)}), bf16[64,32,128]{2,0,1:T(8,128)(2,1)S(1)}, u32[]{:S(2)}, u32[]{:S(2)}) %all-to-all-start.2) | async-done | bytes 524320 | tf_op jit(solution)/shard_map/all_to_all | solution.py:131
  314.4 1.5 convert_element_type.229
  (56 shorter events, 9.3 us)
Async XLA Ops:
  7.2 1.1 copy-start
  7.2 27.0 %copy-start.12 = (bf16[1,128,2048]{2,1,0:T(8,128)(2,1)S(1)}, bf16[1,128,2048]{2,1,0:T(8,128)(2,1)}, u32[]{:S(2)}) copy-start(bf16[1,128,2048]{2,1,0:T(8,128)(2,1)} %param.9) | copy-start | bytes 1572868
  8.9 22.6 %all-to-all-start = ((bf16[32,8,128]{2,1,0:T(8,128)(2,1)}), bf16[32,8,128]{2,1,0:T(8,128)(2,1)S(1)}, u32[]{:S(2)}, u32[]{:S(2)}) async-start(bf16[32,8,128]{2,1,0:T(8,128)(2,1)} %constant_dynamic-slice_fusion), calls=%async_computation | async-start | bytes 131072 | tf_op jit(solution)/shard_map/all_to_all | solution.py:108
  21.6 52.6 %all-gather.5.cloned.1.call-start = ((), (), s32[]{:S(2)}) async-start(), calls=%async_computation.7 | async-start | bytes 1179648 | tf_op jit(solution)/shard_map/all_gather | solution.py:115
  35.2 26.0 %all-to-all-start.3 = ((bf16[32,64,128]{2,1,0:T(8,128)(2,1)}), bf16[32,64,128]{2,1,0:T(8,128)(2,1)S(1)}, u32[]{:S(2)}, u32[]{:S(2)}) async-start(bf16[32,64,128]{2,1,0:T(8,128)(2,1)} %bitcast.24), calls=%async_computation.3 | async-start | bytes 1048576 | tf_op jit(solution)/shard_map/all_to_all | solution.py:106
  39.2 74.2 %all-gather.3.cloned.1.call-start = ((), (), s32[]{:S(2)}) async-start(), calls=%async_computation.6 | async-start | bytes 1179648 | tf_op jit(solution)/shard_map/all_gather | solution.py:112
  113.3 4.6 %copy-start.2 = (f32[64,64,128]{2,1,0:T(8,128)S(1)}, f32[64,64,128]{2,1,0:T(8,128)}, u32[]{:S(2)}) copy-start(f32[64,64,128]{2,1,0:T(8,128)} %fusion.50) | copy-start | bytes 6291460
  113.3 4.6 %copy-start.6 = (bf16[64,64,128]{2,1,0:T(8,128)(2,1)S(1)}, bf16[64,64,128]{2,1,0:T(8,128)(2,1)}, u32[]{:S(2)}) copy-start(bf16[64,64,128]{2,1,0:T(8,128)(2,1)} %all-gather.5.cloned.1.call-done) | copy-start | bytes 3145732
  113.3 4.6 %copy-start.8 = (bf16[64,64,128]{2,1,0:T(8,128)(2,1)S(1)}, bf16[64,64,128]{2,1,0:T(8,128)(2,1)}, u32[]{:S(2)}) copy-start(bf16[64,64,128]{2,1,0:T(8,128)(2,1)} %all-gather.3.cloned.1.call-done) | copy-start | bytes 3145732
  128.2 18.9 %copy-start.13 = (s32[1,128]{1,0:T(1,128)S(1)}, s32[1,128]{1,0:T(1,128)}, u32[]{:S(2)}) copy-start(s32[1,128]{1,0:T(1,128)} %param.14) | copy-start | bytes 1540
  128.2 91.5 %copy-start.14 = (f32[16]{0:T(128)S(1)}, f32[16]{0:T(128)}, u32[]{:S(2)}) copy-start(f32[16]{0:T(128)} %param.15) | copy-start | bytes 196
  128.2 91.5 %copy-start.15 = (s32[1,128]{1,0:T(1,128)S(1)}, s32[1,128]{1,0:T(1,128)}, u32[]{:S(2)}) copy-start(s32[1,128]{1,0:T(1,128)} %param.13) | copy-start | bytes 1540
  129.2 90.6 %all-to-all-start.4 = ((bf16[64,32,128]{2,0,1:T(8,128)(2,1)}), bf16[64,32,128]{2,0,1:T(8,128)(2,1)S(1)}, u32[]{:S(2)}, u32[]{:S(2)}) async-start(bf16[64,32,128]{2,0,1:T(8,128)(2,1)} %copy.38), calls=%async_computation.4 | async-start | bytes 1048576 | tf_op jit(solution)/shard_map/all_to_all | solution.py:130
  143.7 170.7 %reduce-scatter.2.cloned.1.call-start = ((), (), s32[]{:S(2)}) async-start(), calls=%async_computation.8 | async-start | bytes 589824 | tf_op jit(solution)/shard_map/reduce_scatter | solution.py:141
  254.0 2.2 copy-start.3
  256.2 4.1 %copy-start.4 = (f32[64,64,128]{2,1,0:T(8,128)}, f32[64,64,128]{2,1,0:T(8,128)S(1)}, u32[]{:S(2)}) copy-start(f32[64,64,128]{2,1,0:T(8,128)S(1)} %fusion.47) | copy-start | bytes 6291460
  270.7 2.5 copy-start.5
  273.2 4.8 %copy-start.7 = (bf16[64,64,128]{2,1,0:T(8,128)(2,1)S(1)}, bf16[64,64,128]{2,1,0:T(8,128)(2,1)}, u32[]{:S(2)}) copy-start(bf16[64,64,128]{2,1,0:T(8,128)(2,1)} %all-gather.5.cloned.1.call-done) | copy-start | bytes 3145732
  273.2 4.8 %copy-start.9 = (bf16[64,64,128]{2,1,0:T(8,128)(2,1)S(1)}, bf16[64,64,128]{2,1,0:T(8,128)(2,1)}, u32[]{:S(2)}) copy-start(bf16[64,64,128]{2,1,0:T(8,128)(2,1)} %all-gather.3.cloned.1.call-done) | copy-start | bytes 3145732
  273.3 4.8 %copy-start.10 = (f32[64,64,128]{2,1,0:T(8,128)S(1)}, f32[64,64,128]{2,1,0:T(8,128)}, u32[]{:S(2)}) copy-start(f32[64,64,128]{2,1,0:T(8,128)} %get-tuple-element.16) | copy-start | bytes 6291460
  286.3 29.6 %copy-start.1 = (bf16[2048,128]{1,0:T(8,128)(2,1)S(1)}, bf16[2048,128]{1,0:T(8,128)(2,1)}, u32[]{:S(2)}) copy-start(bf16[2048,128]{1,0:T(8,128)(2,1)} %param.11) | copy-start | bytes 1572868
  288.1 5.9 %copy-start.11 = (bf16[128,2048]{0,1:T(8,128)(2,1)S(1)}, bf16[128,2048]{0,1:T(8,128)(2,1)}, u32[]{:S(2)}) copy-start(bf16[128,2048]{0,1:T(8,128)(2,1)} %get-tuple-element.14) | copy-start | bytes 1572868
  289.1 24.2 %all-to-all-start.2 = ((bf16[64,32,128]{2,0,1:T(8,128)(2,1)}), bf16[64,32,128]{2,0,1:T(8,128)(2,1)S(1)}, u32[]{:S(2)}, u32[]{:S(2)}) async-start(bf16[64,32,128]{2,0,1:T(8,128)(2,1)} %copy.35), calls=%async_computation.2 | async-start | bytes 1048576 | tf_op jit(solution)/shard_map/all_to_all | solution.py:131
Sparse Core Ops, SparseCore 0:
  34.3 36.0 all-gather.4
  72.8 40.4 all-gather.2
  273.4 33.0 reduce-scatter.1
where the time goes:
time: 326 us; the launch traced here: 323 us
  blocking collectives  97.7 us (30%)
  waiting for transfers between devices  86.4 us (27%)
  matrix products  71.8 us (22%)
  starting transfers between devices  36.3 us (11%)
  between operations  14.4 us (4%)
  local copies, waits for them, and re-layouts  11.9 us (4%)
  other arithmetic  4.06 us (1%)
    psum x1, blocking collectives, local(): counts = lax.psum(jnp.sum(doc_hot, axis=0), 'ctx')  72.4 us
    all_gather x1, waiting for transfers between devices, local(): lax.all_gather(share_re.astype(jnp.bfloat16), 'dp', axis=0, tiled=True)  39.1 us
    all_to_all x1, blocking collectives, local(): lax.all_to_all(grad_slab, 'ctx', split_axis=0, concat_axis=1, tiled=True)  25.3 us
    all_to_all x1, waiting for transfers between devices, local(): lax.all_to_all(input_slab, 'ctx', split_axis=0, concat_axis=1, tiled=True)  19.2 us
    all_to_all x1, waiting for transfers between devices, local(): lax.all_to_all((back + skip_local * grad_full).astype(jnp.bfloat16), 'ctx...  18.3 us
    all_to_all x1, starting transfers between devices, local(): lax.all_to_all(mixed_pen, 'ctx', split_axis=1, concat_axis=0, tiled=True)  14.5 us
    all_to_all x1, starting transfers between devices, local(): lax.all_to_all(own_taps, 'ctx', split_axis=0, concat_axis=1, tiled=True)  12.8 us
    dot_general x3, matrix products, inverse(): jnp.einsum('ckm,mn->ckn', spec_im, cos_in, precision=highest)  11.8 us
  transfers between devices with their start and end apart: 7, of which 4 were waited for; matrix products, arithmetic and copies ran while one was open for 12% of the time, Pallas kernels for 0%

commit v1 on v0

v1 whole, which is shorter than its diff:
```python
import functools
import math

import jax
import jax.numpy as jnp
import numpy as np
from jax import lax
from jax.experimental import pallas as pl
from jax.experimental.pallas import tpu as pltpu
from jax.sharding import PartitionSpec as P

MESH = pl.DeviceIdType.MESH
BF = jnp.bfloat16
F32 = jnp.float32
NCTX, NDP, NX = 32, 8, 4
LEN = 4096
GR = 8
CH1, CH2 = 4, 8


def tables():
    k1 = np.arange(32)
    a = np.arange(32)
    b = np.arange(128)
    phi = 2 * math.pi / 128 * ((a[None, :] * (4 * k1[:, None] + 1)) % 128)
    first = np.zeros((64, 128), np.float32)
    first[:, :32] = np.stack([np.cos(phi), -np.sin(phi)], 1).reshape(64, 32)
    last = np.zeros((32, 128), np.float32)
    last[:, :64] = first[:, :32].T / LEN
    alpha = 2 * math.pi / 16384 * ((b[None, :] * (4 * k1[:, None] + 1)) % 16384)
    beta = 2 * math.pi / 128 * ((b[None, :] * b[:, None]) % 128)
    f = lambda v: jnp.asarray(v.astype(np.float32))
    return (
        jnp.asarray(first, BF),
        jnp.asarray(last, BF),
        f(np.cos(alpha)),
        f(np.sin(alpha)),
        f(np.cos(beta)),
        f(np.sin(beta)),
    )


def iota(shape, dim):
    return lax.broadcasted_iota(jnp.int32, shape, dim)


def swap(x):
    return pltpu.roll(x, 64, axis=1)


def kernel(
    grad, sig, gate, taps, skip, lang, docs, dro, first, last, cosa, sina, cosb, sinb,
    d_input, d_gate, d_filter,
    docs_out, docs_all, hall, htime, scale, mats, matst, fone, ftwo, send1, recv1, send2, recv2,
    ybuf, vbuf, qbuf, hspec, xspec, dfs, dfr,
    doc_s, doc_r, tap_s, tap_r, gat_s, gat_r, one_s, one_r, two_s, two_r, df_s, df_r, own,
):
    me = lax.axis_index("ctx")
    dp = lax.axis_index("dp")
    xs = lax.rem(dp, NX)
    zl = dp // NX
    low = iota((16, 128), 1) < 64

    def peer_of(p):
        return lax.rem(me + p, NCTX)

    def dp_of(q):
        return lax.rem(dp + q, NDP)

    def x_of(q):
        return zl * NX + lax.rem(xs + q, NX)

    barrier = pltpu.get_barrier_semaphore()

    @pl.loop(1, NCTX)
    def _(p):
        pl.semaphore_signal(barrier, inc=1, device_id={"ctx": peer_of(p)}, device_id_type=MESH)

    @pl.loop(1, NDP)
    def _(q):
        pl.semaphore_signal(barrier, inc=1, device_id={"dp": dp_of(q)}, device_id_type=MESH)

    docs_row = docs[...]
    docs_out[...] = jnp.broadcast_to(docs_row, (8, 128))
    docs_all[me] = jnp.broadcast_to(docs_row, (8, 128))
    pl.semaphore_wait(barrier, NCTX - 1 + NDP - 1)

    @pl.loop(1, NCTX)
    def _(p):
        peer = peer_of(p)
        pltpu.make_async_remote_copy(
            docs_out, docs_all.at[me], doc_s, doc_r, device_id={"ctx": peer}, device_id_type=MESH
        ).start()

    def tap_rows(j):
        return taps.at[pl.ds(pl.multiple_of(64 * j + 16 * xs, 16), 16), :]

    @pl.loop(1, NCTX)
    def _(p):
        peer = peer_of(p)
        pltpu.make_async_remote_copy(
            tap_rows(peer), hall.at[xs, me], tap_s, tap_r, device_id={"ctx": peer}, device_id_type=MESH
        ).start()

    own_taps = pltpu.make_async_copy(tap_rows(me), hall.at[xs, me], own.at[0])
    own_taps.start()

    def column(row):
        return jnp.broadcast_to(row.astype(F32), (128, 128)).T

    own_docs = column(docs_row)
    own_lang = column(lang[...])
    weight = jnp.zeros((128, 128), F32)
    for group in range(16):
        weight = jnp.where(own_lang == float(group), dro[group], weight)
    pltpu.make_async_copy(docs_all.at[0:31], docs_all.at[0:31], doc_r).wait()

    def count(a, total):
        row = jnp.broadcast_to(docs_all[a][0:1].astype(F32), (128, 128))
        return total + jnp.where(row == own_docs, 1.0, 0.0)

    hits = lax.fori_loop(0, NCTX, count, jnp.zeros((128, 128), F32))
    doc_len = jnp.sum(hits, axis=1, keepdims=True)
    scale[...] = weight * 256.0 / (doc_len + 128.0)

    for m in range(16):
        cols = slice(128 * m, 128 * m + 128)

        @pl.loop(0, GR)
        def _(g):
            rows = pl.ds(pl.multiple_of(16 * g, 16), 16)
            u = sig[0, rows, cols].astype(F32)
            dy = grad[0, rows, cols].astype(F32) * scale[rows, :]
            dz = dy * gate[0, rows, cols].astype(F32)
            send1[g, 2 * m] = jnp.where(low, u, swap(dz)).astype(BF)
            send1[g, 2 * m + 1] = jnp.where(low, swap(u), dz).astype(BF)

    per1 = GR // CH1

    def send_in(ch):
        span = slice(per1 * ch, per1 * ch + per1)

        @pl.loop(1, NCTX)
        def _(p):
            peer = peer_of(p)
            pltpu.make_async_remote_copy(
                send1.at[span, peer], recv1.at[span, me], one_s.at[ch], one_r.at[ch],
                device_id={"ctx": peer}, device_id_type=MESH,
            ).start()

    own_one = pltpu.make_async_copy(send1.at[:, me], recv1.at[:, me], own.at[1])
    own_one.start()
    send_in(0)
    own_taps.wait()
    pltpu.make_async_copy(hall.at[0, 0:31], hall.at[0, 0:31], tap_r).wait()

    @pl.loop(1, NX)
    def _(q):
        pltpu.make_async_remote_copy(
            hall.at[xs], hall.at[xs], gat_s, gat_r, device_id={"dp": x_of(q)}, device_id_type=MESH
        ).start()

    for ch in range(1, CH1):
        send_in(ch)

    def expand(small, rows, cols):
        left = (iota((rows, small.shape[0]), 0) // 16 == iota((rows, small.shape[0]), 1)).astype(F32).astype(BF)
        right = (iota((128, cols), 1) // 16 == iota((128, cols), 0)).astype(F32).astype(BF)
        tall = jnp.dot(left, small, preferred_element_type=F32).astype(BF)
        wide = jnp.dot(tall, right, preferred_element_type=F32)
        keep = lax.rem(iota((rows, cols), 0), 16) == lax.rem(iota((rows, cols), 1), 16)
        return jnp.where(keep, wide, 0.0).astype(BF)

    fone[...] = expand(first[...], 1024, 512)
    ftwo[...] = expand(last[...], 512, 1024)

    @pl.loop(0, 32)
    def _(k):
        ca, sa = cosa[pl.ds(k, 1), :], sina[pl.ds(k, 1), :]
        co = ca * cosb[...] - sa * sinb[...]
        si = sa * cosb[...] + ca * sinb[...]
        mats[k, 0:128, 0:128] = co.astype(BF)
        mats[k, 0:128, 128:256] = si.astype(BF)
        mats[k, 128:256, 0:128] = (-si).astype(BF)
        mats[k, 128:256, 128:256] = co.astype(BF)
        cot, sit = co.T, si.T
        matst[k, 0:128, 0:128] = cot.astype(BF)
        matst[k, 0:128, 128:256] = (-sit).astype(BF)
        matst[k, 128:256, 0:128] = sit.astype(BF)
        matst[k, 128:256, 128:256] = cot.astype(BF)

    def stage_one(x, g):
        y = jnp.dot(fone[...], x.reshape(512, 128), preferred_element_type=F32)
        ybuf[:, :, g] = y.astype(BF).reshape(32, 2, 16, 128)

    def stage_two(k):
        return jnp.dot(mats[k], ybuf[k].reshape(256, 128), preferred_element_type=F32)

    pltpu.make_async_copy(hall.at[0:3], hall.at[0:3], gat_r).wait()

    @pl.loop(0, NCTX)
    def _(a):
        block = hall[:, a].reshape(64, 128).astype(F32)
        turned = jnp.concatenate([block, block], axis=0).T
        htime[:, a] = turned.astype(BF).reshape(8, 16, 128)

    @pl.loop(0, GR)
    def _(g):
        stage_one(htime[g], g)

    wide_low = iota((128, 128), 1) < 64

    @pl.loop(0, 32)
    def _(k):
        s = stage_two(k)
        hspec[k, 0:128] = s[0:128]
        hspec[k, 128:256] = jnp.where(wide_low, s[128:256], -s[128:256])

    own_one.wait()
    for ch in range(CH1):
        part = recv1.at[per1 * ch:per1 * ch + per1, 0:31]
        pltpu.make_async_copy(part, part, one_r.at[ch]).wait()

        @pl.loop(per1 * ch, per1 * ch + per1)
        def _(g):
            stage_one(recv1[g], g)

    @pl.loop(0, 32)
    def _(k):
        s = stage_two(k)
        xspec[k] = s
        sr, si = s[0:128], s[128:256]
        hr, hi = hspec[k, 0:128], hspec[k, 128:256]
        p = jnp.concatenate([sr * hr - si * hi, sr * hi + si * hr], axis=0).astype(BF)
        v = jnp.dot(matst[k], p, preferred_element_type=F32).astype(BF).reshape(2, 8, 16, 128)
        vbuf[:, k, 0] = v[0]
        vbuf[:, k, 1] = v[1]

    gain = skip[pl.ds(me // 2, 1), :]
    turned_gain = pltpu.roll(jnp.broadcast_to(gain, (8, 128)), 64, axis=1)[0:1]
    low_row = iota((1, 128), 1) < 64
    even = jnp.where(low_row, gain, turned_gain)
    odd = jnp.where(low_row, turned_gain, gain)
    parity = lax.rem(me, 2).astype(F32)
    gain2 = even * (1.0 - parity) + odd * parity

    per2 = GR // CH2
    for ch in range(CH2):
        @pl.loop(per2 * ch, per2 * ch + per2)
        def _(g):
            o = jnp.dot(ftwo[...], vbuf[g].reshape(1024, 128), preferred_element_type=F32)
            o = o + gain2 * recv1[g].reshape(512, 128).astype(F32)
            send2[g] = o.astype(BF).reshape(32, 16, 128)

        span = slice(per2 * ch, per2 * ch + per2)

        @pl.loop(1, NCTX)
        def _(p):
            peer = peer_of(p)
            pltpu.make_async_remote_copy(
                send2.at[span, peer], recv2.at[span, me], two_s.at[ch], two_r.at[ch],
                device_id={"ctx": peer}, device_id_type=MESH,
            ).start()

    own_two = pltpu.make_async_copy(send2.at[:, me], recv2.at[:, me], own.at[2])
    own_two.start()

    @pl.loop(0, 32)
    def _(k):
        s = xspec[k]
        sr, si = s[0:128], s[128:256]
        gr, gi = swap(sr), swap(si)
        q = jnp.concatenate([sr * gr + si * gi, sr * gi - si * gr], axis=0).astype(BF)
        v = jnp.dot(matst[k], q, preferred_element_type=F32).reshape(2, 2, 64, 128)
        for c in range(2):
            both = jnp.where(iota((64, 128), 1) < 64, v[c, 0], swap(v[c, 1]))
            qbuf[:, k, c] = both.astype(BF).reshape(4, 16, 128)

    @pl.loop(0, 4)
    def _(g):
        o = jnp.dot(ftwo[...], qbuf[g].reshape(1024, 128), preferred_element_type=F32)
        dfs[:, g] = o.astype(BF).reshape(8, 4, 16, 128)

    @pl.loop(1, NDP)
    def _(q):
        other = dp_of(q)
        pltpu.make_async_remote_copy(
            dfs.at[other], dfr.at[dp], df_s, df_r, device_id={"dp": other}, device_id_type=MESH
        ).start()

    own_df = pltpu.make_async_copy(dfs.at[dp], dfr.at[dp], own.at[3])
    own_df.start()

    own_two.wait()
    for ch in range(CH2):
        part = recv2.at[per2 * ch:per2 * ch + per2, 0:31]
        pltpu.make_async_copy(part, part, two_r.at[ch]).wait()

        @pl.loop(per2 * ch, per2 * ch + per2)
        def _(g):
            rows = pl.ds(pl.multiple_of(16 * g, 16), 16)
            factor = scale[rows, :]
            for m in range(16):
                cols = slice(128 * m, 128 * m + 128)
                left, right = recv2[g, 2 * m].astype(F32), recv2[g, 2 * m + 1].astype(F32)
                z = jnp.where(low, left, swap(right))
                d_input[0, rows, cols] = jnp.where(low, swap(left), right).astype(BF)
                d_gate[0, rows, cols] = (grad[0, rows, cols].astype(F32) * factor * z).astype(BF)

    own_df.wait()
    pltpu.make_async_copy(dfr.at[0:7], dfr.at[0:7], df_r).wait()
    for a in range(4):
        total = dfr[0, :, a].astype(F32)
        for r in range(1, NDP):
            total = total + dfr[r, :, a].astype(F32)
        turned = total.reshape(64, 128).T
        d_filter[:, 128 * a:128 * a + 64] = turned[0:64]
        d_filter[:, 128 * a + 64:128 * a + 128] = turned[64:128]

    pltpu.make_async_copy(docs_all.at[0:31], docs_all.at[0:31], doc_s).wait()
    pltpu.make_async_copy(hall.at[0, 0:31], hall.at[0, 0:31], tap_s).wait()
    pltpu.make_async_copy(hall.at[0:3], hall.at[0:3], gat_s).wait()
    for ch in range(CH1):
        part = send1.at[per1 * ch:per1 * ch + per1, 0:31]
        pltpu.make_async_copy(part, part, one_s.at[ch]).wait()
    for ch in range(CH2):
        part = send2.at[per2 * ch:per2 * ch + per2, 0:31]
        pltpu.make_async_copy(part, part, two_s.at[ch]).wait()
    pltpu.make_async_copy(dfs.at[0:7], dfs.at[0:7], df_s).wait()


def local(grad_out, saved_input, gate_value, filter_taps, skip_gain, lang_ids, doc_ids, dro_weight):
    vmem = pl.BlockSpec(memory_space=pltpu.VMEM)
    dma = pltpu.SemaphoreType.DMA
    token = jax.ShapeDtypeStruct((1, 128, 2048), BF)
    return pl.pallas_call(
        kernel,
        out_shape=(token, token, jax.ShapeDtypeStruct((64, 512), F32)),
        in_specs=[vmem] * 7 + [pl.BlockSpec(memory_space=pltpu.SMEM)] + [vmem] * 6,
        out_specs=(vmem, vmem, vmem),
        scratch_shapes=[
            pltpu.VMEM((8, 128), jnp.int32),
            pltpu.VMEM((NCTX, 8, 128), jnp.int32),
            pltpu.VMEM((NX, NCTX, 16, 128), BF),
            pltpu.VMEM((GR, NCTX, 16, 128), BF),
            pltpu.VMEM((128, 128), F32),
            pltpu.VMEM((32, 256, 256), BF),
            pltpu.VMEM((32, 256, 256), BF),
            pltpu.VMEM((1024, 512), BF),
            pltpu.VMEM((512, 1024), BF),
            pltpu.VMEM((GR, NCTX, 16, 128), BF),
            pltpu.VMEM((GR, NCTX, 16, 128), BF),
            pltpu.VMEM((GR, NCTX, 16, 128), BF),
            pltpu.VMEM((GR, NCTX, 16, 128), BF),
            pltpu.VMEM((32, 2, GR, 16, 128), BF),
            pltpu.VMEM((GR, 32, 2, 16, 128), BF),
            pltpu.VMEM((4, 32, 2, 16, 128), BF),
            pltpu.VMEM((32, 256, 128), F32),
            pltpu.VMEM((32, 256, 128), F32),
            pltpu.VMEM((NDP, 4, 4, 16, 128), BF),
            pltpu.VMEM((NDP, 4, 4, 16, 128), BF),
            dma, dma, dma, dma, dma, dma,
            dma((CH1,)), dma((CH1,)), dma((CH2,)), dma((CH2,)),
            dma, dma, dma((4,)),
        ],
        compiler_params=pltpu.CompilerParams(
            collective_id=0, has_side_effects=True, vmem_limit_bytes=56 << 20
        ),
        name="hyena_backward",
    )(
        grad_out, saved_input, gate_value, filter_taps, skip_gain.reshape(16, 128), lang_ids, doc_ids, dro_weight,
        *tables(),
    )


def solution(mesh):
    return jax.shard_map(
        local,
        mesh=mesh,
        in_specs=(
            P("dp", "ctx", None), P("dp", "ctx", None), P("dp", "ctx", None), P(None, "ctx"),
            P(), P("dp", "ctx"), P("dp", "ctx"), P(),
        ),
        out_specs=(P("dp", "ctx", None), P("dp", "ctx", None), P("ctx", "dp")),
        check_vma=False,
    )
```

time: 326 us -> 107 us (0.33)
  Pallas kernels: 0 us -> 102 us
  blocking collectives: 97.7 us -> 0 us
  waiting for transfers between devices: 86.4 us -> 0 us
  matrix products: 71.8 us -> 0 us
  starting transfers between devices: 36.3 us -> 0 us
  between operations: 14.4 us -> 0.65 us
  local copies, waits for them, and re-layouts: 11.9 us -> 3.62 us
  other arithmetic: 4.06 us -> 0 us
    pallas_call x0 -> x1, Pallas kernels: none -> 102 us  [local(): pl.pallas_call(kernel, out_shape=(token, token, jax.ShapeDtypeStruct((64,...]
    psum x1 -> x0, blocking collectives: 72.4 us -> none  [local(): counts = lax.psum(jnp.sum(doc_hot, axis=0), 'ctx')]
    dot_general x36 -> x0, matrix products: 71.8 us -> none  [the longest x3 11.8 us: inverse(): jnp.einsum('ckm,mn->ckn', spec_im, cos_in, precision=highest)]
    all_to_all x4 -> x0, waiting for transfers between devices: 47.2 us -> none  [the longest x1 19.2 us: local(): lax.all_to_all(input_slab, 'ctx', split_axis=0, concat_axis=1, tiled=True)]
    all_gather x2 -> x0, waiting for transfers between devices: 39.1 us -> none  [the longest x1 39.1 us: local(): lax.all_gather(share_re.astype(jnp.bfloat16), 'dp', axis=0, tiled=True)]
    all_to_all x4 -> x0, starting transfers between devices: 36 us -> none  [the longest x1 14.5 us: local(): lax.all_to_all(mixed_pen, 'ctx', split_axis=1, concat_axis=0, tiled=True)]
    all_to_all x1 -> x0, blocking collectives: 25.3 us -> none  [local(): lax.all_to_all(grad_slab, 'ctx', split_axis=0, concat_axis=1, tiled=True)]
    unnamed x38 -> x7, local copies, waits for them, and re-layouts: 8.47 us -> 3.62 us
  transfers between devices with their start and end apart: 7 -> 0, of which waited for: 4 -> 0; matrix products, arithmetic and copies ran while one was open for 12% -> 0% of each run, Pallas kernels for 0% -> 0%
where the time goes in v1:
time: 107 us; the launch traced here: 106 us
  Pallas kernels  102 us (95%)
  local copies, waits for them, and re-layouts  3.62 us (3%)
    pallas_call x1, Pallas kernels, local(): pl.pallas_call(kernel, out_shape=(token, token, jax.ShapeDtypeStruct((64,...  102 us
    unnamed x7, local copies, waits for them, and re-layouts  3.62 us

profile of v1, /device:TPU:1, one launch (start us, length us, event | category | flops | bytes accessed | tf_op | source)
XLA Modules:
  0.0 105.9 jit_solution(13511337570426557461)
XLA Ops:
  0.6 101.7 %hyena_backward.1 = (bf16[1,128,2048]{2,1,0:T(8,128)(2,1)}, bf16[1,128,2048]{2,1,0:T(8,128)(2,1)}, f32[64,512]{1,0:T(8,128)}) custom-call(bf16[1,128,2048]{2,1,0:T(8,128)(2,1)} %grad.1, bf16[1,128,2048]{2,1,0:T(8,128)(2,1)} %sig.1, bf16[1,128,2048]{2,1,0:T(8,128)(2,1)} %gate.1, bf16[2048,128]{1,0:T(8,128)(2,1)} %taps.1, f32[16,128]{1,0:T(8,128)} %bitcast.1, ...), custom_call_target="tpu_custom_call" | custom-call | tf_op jit(solution)/shard_map/hyena_backward/pallas_call | solution.py:336
  102.3 0.0 copy-start
  102.3 1.9 %copy.20 = bf16[1,128,2048]{2,1,0:T(8,128)(2,1)} copy(bf16[1,128,2048]{2,1,0:T(8,128)(2,1)} %get-tuple-element.6) | data formatting | bytes 1048576
  104.3 0.0 copy-done
  104.3 0.0 copy-start.1
  104.3 0.8 copy.21
  105.1 0.2 copy-done.1
  105.3 0.7 copy.22
Async XLA Ops:
  102.3 2.0 %copy-start = (bf16[1,128,2048]{2,1,0:T(8,128)(2,1)S(1)}, bf16[1,128,2048]{2,1,0:T(8,128)(2,1)}, u32[]{:S(2)}) copy-start(bf16[1,128,2048]{2,1,0:T(8,128)(2,1)} %get-tuple-element.7) | copy-start | bytes 1572868
  104.3 1.0 copy-start.1

commit v2 on v1

--- a/solution.py
+++ b/solution.py
@@ -15,7 +15,10 @@
 NCTX, NDP, NX = 32, 8, 4
 LEN = 4096
 GR = 8
-CH1, CH2 = 4, 8
+CU, CD, CO = 2, 4, 8
+UN = 8
+UQ = 4
+SPLIT = 4
 
 
 def tables():
@@ -51,9 +54,9 @@
 def kernel(
     grad, sig, gate, taps, skip, lang, docs, dro, first, last, cosa, sina, cosb, sinb,
     d_input, d_gate, d_filter,
-    docs_out, docs_all, hall, htime, scale, mats, matst, fone, ftwo, send1, recv1, send2, recv2,
+    docs_out, docs_all, hall, htime, scale, mats, matst, fone, ftwo, sendu, recvu, sendd, recvd, xin, send2, recv2,
     ybuf, vbuf, qbuf, hspec, xspec, dfs, dfr,
-    doc_s, doc_r, tap_s, tap_r, gat_s, gat_r, one_s, one_r, two_s, two_r, df_s, df_r, own,
+    doc_s, doc_r, tap_s, tap_r, gat_s, gat_r, u_s, u_r, d_s, d_r, two_s, two_r, df_s, df_r, own,
 ):
     me = lax.axis_index("ctx")
     dp = lax.axis_index("dp")
@@ -80,9 +83,23 @@
     def _(q):
         pl.semaphore_signal(barrier, inc=1, device_id={"dp": dp_of(q)}, device_id_type=MESH)
 
+    def pair_store(dst, g, m, first_half, second_half):
+        dst[g, 2 * m] = jnp.where(low, first_half, swap(second_half)).astype(BF)
+        dst[g, 2 * m + 1] = jnp.where(low, swap(first_half), second_half).astype(BF)
+
+    def rows_of(g):
+        return pl.ds(pl.multiple_of(16 * g, 16), 16)
+
     docs_row = docs[...]
     docs_out[...] = jnp.broadcast_to(docs_row, (8, 128))
     docs_all[me] = jnp.broadcast_to(docs_row, (8, 128))
+
+    @pl.loop(0, 4)
+    def _(g):
+        for m in range(16):
+            cols = slice(128 * m, 128 * m + 128)
+            pair_store(sendu, g, m, sig[0, rows_of(g), cols].astype(F32), sig[0, rows_of(g + 4), cols].astype(F32))
+
     pl.semaphore_wait(barrier, NCTX - 1 + NDP - 1)
 
     @pl.loop(1, NCTX)
@@ -105,6 +122,25 @@
     own_taps = pltpu.make_async_copy(tap_rows(me), hall.at[xs, me], own.at[0])
     own_taps.start()
 
+    def spread(src, dst, chunk, chunks, sems, semr):
+        per = src.shape[0] // chunks
+        span = slice(per * chunk, per * chunk + per)
+
+        @pl.loop(1, NCTX)
+        def _(p):
+            peer = peer_of(p)
+            pltpu.make_async_remote_copy(
+                src.at[span, peer], dst.at[span, me], sems.at[chunk], semr.at[chunk],
+                device_id={"ctx": peer}, device_id_type=MESH,
+            ).start()
+
+    def await_all(buf, chunk, chunks, sem):
+        per = buf.shape[0] // chunks
+        part = buf.at[per * chunk:per * chunk + per, 0:31]
+        pltpu.make_async_copy(part, part, sem.at[chunk]).wait()
+
+    spread(sendu, recvu, 0, CU, u_s, u_r)
+
     def column(row):
         return jnp.broadcast_to(row.astype(F32), (128, 128)).T
 
@@ -123,34 +159,6 @@
     doc_len = jnp.sum(hits, axis=1, keepdims=True)
     scale[...] = weight * 256.0 / (doc_len + 128.0)
 
-    for m in range(16):
-        cols = slice(128 * m, 128 * m + 128)
-
-        @pl.loop(0, GR)
-        def _(g):
-            rows = pl.ds(pl.multiple_of(16 * g, 16), 16)
-            u = sig[0, rows, cols].astype(F32)
-            dy = grad[0, rows, cols].astype(F32) * scale[rows, :]
-            dz = dy * gate[0, rows, cols].astype(F32)
-            send1[g, 2 * m] = jnp.where(low, u, swap(dz)).astype(BF)
-            send1[g, 2 * m + 1] = jnp.where(low, swap(u), dz).astype(BF)
-
-    per1 = GR // CH1
-
-    def send_in(ch):
-        span = slice(per1 * ch, per1 * ch + per1)
-
-        @pl.loop(1, NCTX)
-        def _(p):
-            peer = peer_of(p)
-            pltpu.make_async_remote_copy(
-                send1.at[span, peer], recv1.at[span, me], one_s.at[ch], one_r.at[ch],
-                device_id={"ctx": peer}, device_id_type=MESH,
-            ).start()
-
-    own_one = pltpu.make_async_copy(send1.at[:, me], recv1.at[:, me], own.at[1])
-    own_one.start()
-    send_in(0)
     own_taps.wait()
     pltpu.make_async_copy(hall.at[0, 0:31], hall.at[0, 0:31], tap_r).wait()
 
@@ -160,8 +168,27 @@
             hall.at[xs], hall.at[xs], gat_s, gat_r, device_id={"dp": x_of(q)}, device_id_type=MESH
         ).start()
 
-    for ch in range(1, CH1):
-        send_in(ch)
+    for ch in range(1, CU):
+        spread(sendu, recvu, ch, CU, u_s, u_r)
+
+    for ch in range(CD):
+        @pl.loop(4 // CD * ch, 4 // CD * ch + 4 // CD)
+        def _(g):
+            for m in range(16):
+                cols = slice(128 * m, 128 * m + 128)
+                halves = []
+                for h in range(2):
+                    rows = rows_of(g + 4 * h)
+                    dy = grad[0, rows, cols].astype(F32) * scale[rows, :]
+                    halves.append(dy * gate[0, rows, cols].astype(F32))
+                pair_store(sendd, g, m, *halves)
+
+        spread(sendd, recvd, ch, CD, d_s, d_r)
+
+    own_u = pltpu.make_async_copy(sendu.at[:, me], recvu.at[:, me], own.at[1])
+    own_u.start()
+    own_d = pltpu.make_async_copy(sendd.at[:, me], recvd.at[:, me], own.at[4])
+    own_d.start()
 
     def expand(small, rows, cols):
         left = (iota((rows, small.shape[0]), 0) // 16 == iota((rows, small.shape[0]), 1)).astype(F32).astype(BF)
@@ -210,22 +237,32 @@
 
     wide_low = iota((128, 128), 1) < 64
 
-    @pl.loop(0, 32)
+    @pl.loop(0, 32, unroll=UQ)
     def _(k):
         s = stage_two(k)
         hspec[k, 0:128] = s[0:128]
         hspec[k, 128:256] = jnp.where(wide_low, s[128:256], -s[128:256])
 
-    own_one.wait()
-    for ch in range(CH1):
-        part = recv1.at[per1 * ch:per1 * ch + per1, 0:31]
-        pltpu.make_async_copy(part, part, one_r.at[ch]).wait()
-
-        @pl.loop(per1 * ch, per1 * ch + per1)
+    own_u.wait()
+    own_d.wait()
+    for ch in range(CU):
+        await_all(recvu, ch, CU, u_r)
+    tall_low = iota((512, 128), 1) < 64
+    for ch in range(CD):
+        await_all(recvd, ch, CD, d_r)
+
+        @pl.loop(4 // CD * ch, 4 // CD * ch + 4 // CD)
         def _(g):
-            stage_one(recv1[g], g)
-
-    @pl.loop(0, 32)
+            u = recvu[g].reshape(512, 128).astype(F32)
+            d = recvd[g].reshape(512, 128).astype(F32)
+            first_half = jnp.where(tall_low, u, swap(d)).astype(BF).reshape(32, 16, 128)
+            second_half = jnp.where(tall_low, swap(u), d).astype(BF).reshape(32, 16, 128)
+            xin[g] = first_half
+            xin[g + 4] = second_half
+            stage_one(first_half, g)
+            stage_one(second_half, g + 4)
+
+    @pl.loop(0, 32, unroll=UN)
     def _(k):
         s = stage_two(k)
         xspec[k] = s
@@ -244,28 +281,21 @@
     parity = lax.rem(me, 2).astype(F32)
     gain2 = even * (1.0 - parity) + odd * parity
 
-    per2 = GR // CH2
-    for ch in range(CH2):
+    per2 = GR // CO
+
+    def send_back(ch):
         @pl.loop(per2 * ch, per2 * ch + per2)
         def _(g):
             o = jnp.dot(ftwo[...], vbuf[g].reshape(1024, 128), preferred_element_type=F32)
-            o = o + gain2 * recv1[g].reshape(512, 128).astype(F32)
+            o = o + gain2 * xin[g].reshape(512, 128).astype(F32)
             send2[g] = o.astype(BF).reshape(32, 16, 128)
 
-        span = slice(per2 * ch, per2 * ch + per2)
-
-        @pl.loop(1, NCTX)
-        def _(p):
-            peer = peer_of(p)
-            pltpu.make_async_remote_copy(
-                send2.at[span, peer], recv2.at[span, me], two_s.at[ch], two_r.at[ch],
-                device_id={"ctx": peer}, device_id_type=MESH,
-            ).start()
-
-    own_two = pltpu.make_async_copy(send2.at[:, me], recv2.at[:, me], own.at[2])
-    own_two.start()
-
-    @pl.loop(0, 32)
+        spread(send2, recv2, ch, CO, two_s, two_r)
+
+    for ch in range(SPLIT):
+        send_back(ch)
+
+    @pl.loop(0, 32, unroll=UQ)
     def _(k):
         s = xspec[k]
         sr, si = s[0:128], s[128:256]
@@ -291,10 +321,15 @@
     own_df = pltpu.make_async_copy(dfs.at[dp], dfr.at[dp], own.at[3])
     own_df.start()
 
+    for ch in range(SPLIT, CO):
+        send_back(ch)
+
+    own_two = pltpu.make_async_copy(send2.at[:, me], recv2.at[:, me], own.at[2])
+    own_two.start()
+
     own_two.wait()
-    for ch in range(CH2):
-        part = recv2.at[per2 * ch:per2 * ch + per2, 0:31]
-        pltpu.make_async_copy(part, part, two_r.at[ch]).wait()
+    for ch in range(CO):
+        await_all(recv2, ch, CO, two_r)
 
         @pl.loop(per2 * ch, per2 * ch + per2)
         def _(g):
@@ -320,12 +355,12 @@
     pltpu.make_async_copy(docs_all.at[0:31], docs_all.at[0:31], doc_s).wait()
     pltpu.make_async_copy(hall.at[0, 0:31], hall.at[0, 0:31], tap_s).wait()
     pltpu.make_async_copy(hall.at[0:3], hall.at[0:3], gat_s).wait()
-    for ch in range(CH1):
-        part = send1.at[per1 * ch:per1 * ch + per1, 0:31]
-        pltpu.make_async_copy(part, part, one_s.at[ch]).wait()
-    for ch in range(CH2):
-        part = send2.at[per2 * ch:per2 * ch + per2, 0:31]
-        pltpu.make_async_copy(part, part, two_s.at[ch]).wait()
+    for ch in range(CU):
+        await_all(sendu, ch, CU, u_s)
+    for ch in range(CD):
+        await_all(sendd, ch, CD, d_s)
+    for ch in range(CO):
+        await_all(send2, ch, CO, two_s)
     pltpu.make_async_copy(dfs.at[0:7], dfs.at[0:7], df_s).wait()
 
 
@@ -348,7 +383,10 @@
             pltpu.VMEM((32, 256, 256), BF),
             pltpu.VMEM((1024, 512), BF),
             pltpu.VMEM((512, 1024), BF),
-            pltpu.VMEM((GR, NCTX, 16, 128), BF),
+            pltpu.VMEM((4, NCTX, 16, 128), BF),
+            pltpu.VMEM((4, NCTX, 16, 128), BF),
+            pltpu.VMEM((4, NCTX, 16, 128), BF),
+            pltpu.VMEM((4, NCTX, 16, 128), BF),
             pltpu.VMEM((GR, NCTX, 16, 128), BF),
             pltpu.VMEM((GR, NCTX, 16, 128), BF),
             pltpu.VMEM((GR, NCTX, 16, 128), BF),
@@ -360,8 +398,8 @@
             pltpu.VMEM((NDP, 4, 4, 16, 128), BF),
             pltpu.VMEM((NDP, 4, 4, 16, 128), BF),
             dma, dma, dma, dma, dma, dma,
-            dma((CH1,)), dma((CH1,)), dma((CH2,)), dma((CH2,)),
-            dma, dma, dma((4,)),
+            dma((CU,)), dma((CU,)), dma((CD,)), dma((CD,)), dma((CO,)), dma((CO,)),
+            dma, dma, dma((5,)),
         ],
         compiler_params=pltpu.CompilerParams(
             collective_id=0, has_side_effects=True, vmem_limit_bytes=56 << 20

time: 107 us -> 88.4 us (0.83)
  Pallas kernels: 102 us -> 84 us
    pallas_call x1, Pallas kernels: 102 us -> 84 us  [local(): pl.pallas_call(kernel, out_shape=(token, token, jax.ShapeDtypeStruct((64,...]
where the time goes in v2:
time: 88.4 us; the launch traced here: 88.3 us
  Pallas kernels  84 us (95%)
  local copies, waits for them, and re-layouts  3.62 us (4%)
    pallas_call x1, Pallas kernels, local(): pl.pallas_call(kernel, out_shape=(token, token, jax.ShapeDtypeStruct((64,...  84 us
    unnamed x7, local copies, waits for them, and re-layouts  3.62 us

profile of v2, /device:TPU:1, one launch (start us, length us, event | category | flops | bytes accessed | tf_op | source)
XLA Modules:
  0.0 88.3 jit_solution(1421711806571425489)
XLA Ops:
  0.6 84.0 %hyena_backward.1 = (bf16[1,128,2048]{2,1,0:T(8,128)(2,1)}, bf16[1,128,2048]{2,1,0:T(8,128)(2,1)}, f32[64,512]{1,0:T(8,128)}) custom-call(bf16[1,128,2048]{2,1,0:T(8,128)(2,1)} %grad.1, bf16[1,128,2048]{2,1,0:T(8,128)(2,1)} %sig.1, bf16[1,128,2048]{2,1,0:T(8,128)(2,1)} %gate.1, bf16[2048,128]{1,0:T(8,128)(2,1)} %taps.1, f32[16,128]{1,0:T(8,128)} %bitcast.1, ...), custom_call_target="tpu_custom_call" | custom-call | tf_op jit(solution)/shard_map/hyena_backward/pallas_call | solution.py:371
  84.7 0.0 copy-start
  84.7 1.9 %copy.20 = bf16[1,128,2048]{2,1,0:T(8,128)(2,1)} copy(bf16[1,128,2048]{2,1,0:T(8,128)(2,1)} %get-tuple-element.6) | data formatting | bytes 1048576
  86.6 0.0 copy-done
  86.6 0.0 copy-start.1
  86.6 0.8 copy.21
  87.4 0.2 copy-done.1
  87.6 0.7 copy.22
Async XLA Ops:
  84.7 2.0 %copy-start = (bf16[1,128,2048]{2,1,0:T(8,128)(2,1)S(1)}, bf16[1,128,2048]{2,1,0:T(8,128)(2,1)}, u32[]{:S(2)}) copy-start(bf16[1,128,2048]{2,1,0:T(8,128)(2,1)} %get-tuple-element.7) | copy-start | bytes 1572868
  86.6 1.0 %copy-start.1 = (f32[64,512]{1,0:T(8,128)S(1)}, f32[64,512]{1,0:T(8,128)}, u32[]{:S(2)}) copy-start(f32[64,512]{1,0:T(8,128)} %get-tuple-element.8) | copy-start | bytes 393220

commit v3 on v2

v3 whole, which is shorter than its diff:
```python
import functools
import math

import jax
import jax.numpy as jnp
import numpy as np
from jax import lax
from jax.experimental import pallas as pl
from jax.experimental.pallas import tpu as pltpu
from jax.sharding import PartitionSpec as P

MESH = pl.DeviceIdType.MESH
BF = jnp.bfloat16
F32 = jnp.float32
NCTX, NDP, NX = 32, 8, 4
LEN = 4096
CC = (2, 2)
FIRST = 1
GR = 8
CI, CO = CC
UN = 8
UQ = 4


def tables():
    k1 = np.arange(32)
    a = np.arange(32)
    b = np.arange(128)
    phi = 2 * math.pi / 128 * ((a[None, :] * (4 * k1[:, None] + 1)) % 128)
    first = np.zeros((64, 128), np.float32)
    first[:, :32] = np.stack([np.cos(phi), -np.sin(phi)], 1).reshape(64, 32)
    last = np.zeros((32, 128), np.float32)
    last[:, :64] = first[:, :32].T / LEN
    alpha = 2 * math.pi / 16384 * ((b[None, :] * (4 * k1[:, None] + 1)) % 16384)
    beta = 2 * math.pi / 128 * ((b[None, :] * b[:, None]) % 128)
    f = lambda v: jnp.asarray(v.astype(np.float32))
    return (
        jnp.asarray(first, BF),
        jnp.asarray(last, BF),
        f(np.cos(alpha)),
        f(np.sin(alpha)),
        f(np.cos(beta)),
        f(np.sin(beta)),
    )


def iota(shape, dim):
    return lax.broadcasted_iota(jnp.int32, shape, dim)


def swap(x):
    return pltpu.roll(x, 64, axis=1)


def kernel(
    grad, sig, gate, taps, skip, lang, docs, dro, first, last, cosa, sina, cosb, sinb,
    d_input, d_gate, d_filter,
    docs_out, docs_all, hall, htime, scale, mats, matst, fone, ftwo, sendu, recvu, sendd, recvd, sendz, recvz,
    sendi, recvi, ybuf, vbuf, qbuf, hspec, uspec, gspec, dfs, dfr, dft, dfq,
    doc_s, doc_r, tap_s, tap_r, gat_s, gat_r, u_s, u_r, d_s, d_r, z_s, z_r, i_s, i_r, df_s, df_r, dq_s, dq_r, own,
):
    me = lax.axis_index("ctx")
    dp = lax.axis_index("dp")
    xs = lax.rem(dp, NX)
    zl = dp // NX
    low = iota((16, 128), 1) < 64

    def peer_of(p):
        return lax.rem(me + p, NCTX)

    def x_of(q):
        return zl * NX + lax.rem(xs + q, NX)

    barrier = pltpu.get_barrier_semaphore()

    @pl.loop(1, NCTX)
    def _(p):
        pl.semaphore_signal(barrier, inc=1, device_id={"ctx": peer_of(p)}, device_id_type=MESH)

    across = lax.rem(dp + NX, NDP)

    @pl.loop(1, NX)
    def _(q):
        pl.semaphore_signal(barrier, inc=1, device_id={"dp": x_of(q)}, device_id_type=MESH)

    pl.semaphore_signal(barrier, inc=1, device_id={"dp": across}, device_id_type=MESH)

    def pair_store(dst, g, m, first_half, second_half):
        dst[g, 2 * m] = jnp.where(low, first_half, swap(second_half)).astype(BF)
        dst[g, 2 * m + 1] = jnp.where(low, swap(first_half), second_half).astype(BF)

    def rows_of(g):
        return pl.ds(pl.multiple_of(16 * g, 16), 16)

    docs_row = docs[...]
    docs_out[...] = docs_row
    docs_all[me] = docs_row

    @pl.loop(0, 4)
    def _(g):
        for m in range(16):
            cols = slice(128 * m, 128 * m + 128)
            pair_store(sendu, g, m, sig[0, rows_of(g), cols].astype(F32), sig[0, rows_of(g + 4), cols].astype(F32))

    pl.semaphore_wait(barrier, NCTX - 1 + NX)

    @pl.loop(1, NCTX)
    def _(p):
        peer = peer_of(p)
        pltpu.make_async_remote_copy(
            docs_out, docs_all.at[me], doc_s, doc_r, device_id={"ctx": peer}, device_id_type=MESH
        ).start()

    def tap_rows(j):
        return taps.at[pl.ds(pl.multiple_of(64 * j + 16 * xs, 16), 16), :]

    @pl.loop(1, NCTX)
    def _(p):
        peer = peer_of(p)
        pltpu.make_async_remote_copy(
            tap_rows(peer), hall.at[xs, me], tap_s, tap_r, device_id={"ctx": peer}, device_id_type=MESH
        ).start()

    own_taps = pltpu.make_async_copy(tap_rows(me), hall.at[xs, me], own.at[0])
    own_taps.start()

    def spread(src, dst, chunk, chunks, sems, semr):
        per = src.shape[0] // chunks
        span = slice(per * chunk, per * chunk + per)

        @pl.loop(1, NCTX)
        def _(p):
            peer = peer_of(p)
            pltpu.make_async_remote_copy(
                src.at[span, peer], dst.at[span, me], sems.at[chunk], semr.at[chunk],
                device_id={"ctx": peer}, device_id_type=MESH,
            ).start()

    def await_all(buf, chunk, chunks, sem):
        per = buf.shape[0] // chunks
        part = buf.at[per * chunk:per * chunk + per, 0:31]
        pltpu.make_async_copy(part, part, sem.at[chunk]).wait()

    spread(sendu, recvu, 0, CI, u_s, u_r)

    own_taps.wait()
    pltpu.make_async_copy(hall.at[0, 0:31], hall.at[0, 0:31], tap_r).wait()

    @pl.loop(1, NX)
    def _(q):
        pltpu.make_async_remote_copy(
            hall.at[xs], hall.at[xs], gat_s, gat_r, device_id={"dp": x_of(q)}, device_id_type=MESH
        ).start()

    for ch in range(1, CI):
        spread(sendu, recvu, ch, CI, u_s, u_r)

    def column(row):
        return jnp.broadcast_to(row.astype(F32), (128, 128)).T

    own_docs = column(docs_row)
    own_lang = column(lang[...])
    weight = jnp.zeros((128, 128), F32)
    for group in range(16):
        weight = jnp.where(own_lang == float(group), dro[group], weight)
    pltpu.make_async_copy(docs_all.at[0:31], docs_all.at[0:31], doc_r).wait()

    def count(a, total):
        row = jnp.broadcast_to(docs_all[a].astype(F32), (128, 128))
        return total + jnp.where(row == own_docs, 1.0, 0.0)

    hits = lax.fori_loop(0, NCTX, count, jnp.zeros((128, 128), F32))
    doc_len = jnp.sum(hits, axis=1, keepdims=True)
    scale[...] = weight * 256.0 / (doc_len + 128.0)

    for ch in range(CI):
        @pl.loop(4 // CI * ch, 4 // CI * ch + 4 // CI)
        def _(g):
            for m in range(16):
                cols = slice(128 * m, 128 * m + 128)
                halves = []
                for h in range(2):
                    rows = rows_of(g + 4 * h)
                    dy = grad[0, rows, cols].astype(F32) * scale[rows, :]
                    halves.append(dy * gate[0, rows, cols].astype(F32))
                pair_store(sendd, g, m, *halves)

        spread(sendd, recvd, ch, CI, d_s, d_r)

    own_u = pltpu.make_async_copy(sendu.at[:, me], recvu.at[:, me], own.at[1])
    own_u.start()
    own_d = pltpu.make_async_copy(sendd.at[:, me], recvd.at[:, me], own.at[4])
    own_d.start()

    def expand(small, rows, cols):
        left = (iota((rows, small.shape[0]), 0) // 16 == iota((rows, small.shape[0]), 1)).astype(F32).astype(BF)
        right = (iota((128, cols), 1) // 16 == iota((128, cols), 0)).astype(F32).astype(BF)
        tall = jnp.dot(left, small, preferred_element_type=F32).astype(BF)
        wide = jnp.dot(tall, right, preferred_element_type=F32)
        keep = lax.rem(iota((rows, cols), 0), 16) == lax.rem(iota((rows, cols), 1), 16)
        return jnp.where(keep, wide, 0.0).astype(BF)

    fone[...] = expand(first[...], 1024, 512)
    ftwo[...] = expand(last[...], 512, 1024)

    @pl.loop(0, 32)
    def _(k):
        ca, sa = cosa[pl.ds(k, 1), :], sina[pl.ds(k, 1), :]
        co = ca * cosb[...] - sa * sinb[...]
        si = sa * cosb[...] + ca * sinb[...]
        mats[k, 0:128, 0:128] = co.astype(BF)
        mats[k, 0:128, 128:256] = si.astype(BF)
        mats[k, 128:256, 0:128] = (-si).astype(BF)
        mats[k, 128:256, 128:256] = co.astype(BF)
        cot, sit = co.T, si.T
        matst[k, 0:128, 0:128] = cot.astype(BF)
        matst[k, 0:128, 128:256] = (-sit).astype(BF)
        matst[k, 128:256, 0:128] = sit.astype(BF)
        matst[k, 128:256, 128:256] = cot.astype(BF)

    def stage_one(x, g):
        y = jnp.dot(fone[...], x.reshape(512, 128), preferred_element_type=F32)
        ybuf[:, :, g] = y.astype(BF).reshape(32, 2, 16, 128)
        ybuf[:, :, g + 4] = swap(y).astype(BF).reshape(32, 2, 16, 128)

    def stage_two(k):
        return jnp.dot(mats[k], ybuf[k].reshape(256, 128), preferred_element_type=F32)

    pltpu.make_async_copy(hall.at[0:3], hall.at[0:3], gat_r).wait()

    @pl.loop(0, NCTX, unroll=2)
    def _(a):
        block = hall[:, a].reshape(64, 128).astype(F32)
        turned = jnp.concatenate([block, swap(block)], axis=0).T
        htime[:, a] = turned[0:64].astype(BF).reshape(4, 16, 128)

    @pl.loop(0, 4)
    def _(g):
        stage_one(htime[g], g)

    @pl.loop(0, 32, unroll=UQ)
    def _(k):
        hspec[k] = stage_two(k)

    gain = skip[pl.ds(me // 2, 1), :]
    turned_gain = pltpu.roll(jnp.broadcast_to(gain, (8, 128)), 64, axis=1)[0:1]
    low_row = iota((1, 128), 1) < 64
    even = jnp.where(low_row, gain, turned_gain)
    odd = jnp.where(low_row, turned_gain, gain)
    parity = lax.rem(me, 2).astype(F32)
    gain2 = even * (1.0 - parity) + odd * parity
    half_low = iota((64, 128), 1) < 64

    def invert(k, p, buf):
        v = jnp.dot(matst[k], p.astype(BF), preferred_element_type=F32).reshape(2, 2, 64, 128)
        for c in range(2):
            both = jnp.where(half_low, v[c, 0], swap(v[c, 1]))
            buf[:, k, c] = both.astype(BF).reshape(4, 16, 128)

    def bring(recv, local_copy, sem):
        local_copy.wait()
        for ch in range(CI):
            await_all(recv, ch, CI, sem)

            @pl.loop(4 // CI * ch, 4 // CI * ch + 4 // CI)
            def _(g):
                stage_one(recv[g], g)

    def send_back(source, send, recv, chunks, sems, semr):
        for ch in chunks:
            @pl.loop(4 // CO * ch, 4 // CO * ch + 4 // CO)
            def _(g):
                o = jnp.dot(ftwo[...], vbuf[g].reshape(1024, 128), preferred_element_type=F32)
                o = o + gain2 * source[g].reshape(512, 128).astype(F32)
                send[g] = o.astype(BF).reshape(32, 16, 128)

            spread(send, recv, ch, CO, sems, semr)

    bring(recvu, own_u, u_r)

    @pl.loop(0, 32, unroll=UN)
    def _(k):
        s = stage_two(k)
        uspec[k] = s
        sr, si = s[0:128], s[128:256]
        hr, hi = hspec[k, 0:128], hspec[k, 128:256]
        invert(k, jnp.concatenate([sr * hr - si * hi, sr * hi + si * hr], axis=0), vbuf)

    send_back(recvu, sendz, recvz, range(CO), z_s, z_r)
    own_z = pltpu.make_async_copy(sendz.at[:, me], recvz.at[:, me], own.at[2])
    own_z.start()

    bring(recvd, own_d, d_r)

    @pl.loop(0, 32, unroll=UN)
    def _(k):
        s = stage_two(k)
        gspec[k] = s
        sr, si = s[0:128], s[128:256]
        hr, hi = hspec[k, 0:128], hspec[k, 128:256]
        invert(k, jnp.concatenate([sr * hr + si * hi, si * hr - sr * hi], axis=0), vbuf)

    send_back(recvd, sendi, recvi, range(FIRST), i_s, i_r)

    @pl.loop(0, 32, unroll=UN)
    def _(k):
        sr, si = gspec[k, 0:128], gspec[k, 128:256]
        ur, ui = uspec[k, 0:128], uspec[k, 128:256]
        invert(k, jnp.concatenate([sr * ur + si * ui, si * ur - sr * ui], axis=0), qbuf)

    @pl.loop(0, 4)
    def _(g):
        o = jnp.dot(ftwo[...], qbuf[g].reshape(1024, 128), preferred_element_type=F32)
        o = o.astype(BF).reshape(2, 4, 4, 16, 128)
        dfs[:, 0, g] = o[0]
        dfs[:, 1, g] = o[1]

    @pl.loop(1, NX)
    def _(q):
        other = lax.rem(xs + q, NX)
        pltpu.make_async_remote_copy(
            dfs.at[other], dfr.at[xs], df_s, df_r, device_id={"dp": x_of(q)}, device_id_type=MESH
        ).start()

    own_df = pltpu.make_async_copy(dfs.at[xs], dfr.at[xs], own.at[3])
    own_df.start()
    send_back(recvd, sendi, recvi, range(FIRST, CO), i_s, i_r)
    own_i = pltpu.make_async_copy(sendi.at[:, me], recvi.at[:, me], own.at[0])
    own_i.start()

    own_df.wait()
    pltpu.make_async_copy(dfr.at[0:3], dfr.at[0:3], df_r).wait()

    def x_sum(zside):
        total = dfr[0, zside].astype(F32)
        for r in range(1, NX):
            total = total + dfr[r, zside].astype(F32)
        return total

    dft[...] = x_sum(1 - zl).astype(BF)
    swap_df = pltpu.make_async_remote_copy(
        dft, dfq, dq_s, dq_r, device_id={"dp": across}, device_id_type=MESH
    )
    swap_df.start()
    own_z.wait()
    own_i.wait()

    def unpair(recv, g, m):
        left, right = recv[g, 2 * m].astype(F32), recv[g, 2 * m + 1].astype(F32)
        return jnp.where(low, left, swap(right)), jnp.where(low, swap(left), right)

    for ch in range(CO):
        await_all(recvz, ch, CO, z_r)

        @pl.loop(4 // CO * ch, 4 // CO * ch + 4 // CO)
        def _(g):
            for m in range(16):
                cols = slice(128 * m, 128 * m + 128)
                for h, z in enumerate(unpair(recvz, g, m)):
                    rows = rows_of(g + 4 * h)
                    d_gate[0, rows, cols] = (grad[0, rows, cols].astype(F32) * scale[rows, :] * z).astype(BF)

    for ch in range(CO):
        await_all(recvi, ch, CO, i_r)

        @pl.loop(4 // CO * ch, 4 // CO * ch + 4 // CO)
        def _(g):
            for m in range(16):
                cols = slice(128 * m, 128 * m + 128)
                for h, v in enumerate(unpair(recvi, g, m)):
                    d_input[0, rows_of(g + 4 * h), cols] = v.astype(BF)

    swap_df.wait_recv()
    final = x_sum(zl) + dfq[...].astype(F32)
    for a in range(4):
        turned = final[:, a].reshape(64, 128).T
        d_filter[:, 128 * a:128 * a + 64] = turned[0:64]
        d_filter[:, 128 * a + 64:128 * a + 128] = turned[64:128]

    pltpu.make_async_copy(docs_all.at[0:31], docs_all.at[0:31], doc_s).wait()
    pltpu.make_async_copy(hall.at[0, 0:31], hall.at[0, 0:31], tap_s).wait()
    pltpu.make_async_copy(hall.at[0:3], hall.at[0:3], gat_s).wait()
    for ch in range(CI):
        await_all(sendu, ch, CI, u_s)
        await_all(sendd, ch, CI, d_s)
    for ch in range(CO):
        await_all(sendz, ch, CO, z_s)
        await_all(sendi, ch, CO, i_s)
    pltpu.make_async_copy(dfs.at[0:3], dfs.at[0:3], df_s).wait()
    swap_df.wait_send()


def local(grad_out, saved_input, gate_value, filter_taps, skip_gain, lang_ids, doc_ids, dro_weight):
    vmem = pl.BlockSpec(memory_space=pltpu.VMEM)
    dma = pltpu.SemaphoreType.DMA
    token = jax.ShapeDtypeStruct((1, 128, 2048), BF)
    return pl.pallas_call(
        kernel,
        out_shape=(token, token, jax.ShapeDtypeStruct((64, 512), F32)),
        in_specs=[vmem] * 7 + [pl.BlockSpec(memory_space=pltpu.SMEM)] + [vmem] * 6,
        out_specs=(vmem, vmem, vmem),
        scratch_shapes=[
            pltpu.VMEM((1, 128), jnp.int32),
            pltpu.VMEM((NCTX, 1, 128), jnp.int32),
            pltpu.VMEM((NX, NCTX, 16, 128), BF),
            pltpu.VMEM((4, NCTX, 16, 128), BF),
            pltpu.VMEM((128, 128), F32),
            pltpu.VMEM((32, 256, 256), BF),
            pltpu.VMEM((32, 256, 256), BF),
            pltpu.VMEM((1024, 512), BF),
            pltpu.VMEM((512, 1024), BF),
            *[pltpu.VMEM((4, NCTX, 16, 128), BF)] * 8,
            pltpu.VMEM((32, 2, GR, 16, 128), BF),
            pltpu.VMEM((4, 32, 2, 16, 128), BF),
            pltpu.VMEM((4, 32, 2, 16, 128), BF),
            pltpu.VMEM((32, 256, 128), F32),
            pltpu.VMEM((32, 256, 128), F32),
            pltpu.VMEM((32, 256, 128), F32),
            pltpu.VMEM((NX, 2, 4, 4, 16, 128), BF),
            pltpu.VMEM((NX, 2, 4, 4, 16, 128), BF),
            pltpu.VMEM((4, 4, 16, 128), BF),
            pltpu.VMEM((4, 4, 16, 128), BF),
            dma, dma, dma, dma, dma, dma,
            *[dma((CI,))] * 4,
            *[dma((CO,))] * 4,
            dma, dma, dma, dma, dma((5,)),
        ],
        compiler_params=pltpu.CompilerParams(
            collective_id=0, has_side_effects=True, vmem_limit_bytes=56 << 20
        ),
        name="hyena_backward",
    )(
        grad_out, saved_input, gate_value, filter_taps, skip_gain.reshape(16, 128), lang_ids, doc_ids, dro_weight,
        *tables(),
    )


def solution(mesh):
    return jax.shard_map(
        local,
        mesh=mesh,
        in_specs=(
            P("dp", "ctx", None), P("dp", "ctx", None), P("dp", "ctx", None), P(None, "ctx"),
            P(), P("dp", "ctx"), P("dp", "ctx"), P(),
        ),
        out_specs=(P("dp", "ctx", None), P("dp", "ctx", None), P("ctx", "dp")),
        check_vma=False,
    )
```

time: 88.4 us -> 75 us (0.85)
  Pallas kernels: 84 us -> 70.6 us
    pallas_call x1, Pallas kernels: 84 us -> 70.6 us  [local(): pl.pallas_call(kernel, out_shape=(token, token, jax.ShapeDtypeStruct((64,...]
where the time goes in v3:
time: 75 us; the launch traced here: 74.8 us
  Pallas kernels  70.6 us (94%)
  local copies, waits for them, and re-layouts  3.62 us (5%)
    pallas_call x1, Pallas kernels, local(): pl.pallas_call(kernel, out_shape=(token, token, jax.ShapeDtypeStruct((64,...  70.6 us
    unnamed x7, local copies, waits for them, and re-layouts  3.62 us

profile of v3, /device:TPU:1, one launch (start us, length us, event | category | flops | bytes accessed | tf_op | source)
XLA Modules:
  0.0 74.8 jit_solution(16555847185091084089)
XLA Ops:
  0.6 70.6 %hyena_backward.1 = (bf16[1,128,2048]{2,1,0:T(8,128)(2,1)}, bf16[1,128,2048]{2,1,0:T(8,128)(2,1)}, f32[64,512]{1,0:T(8,128)}) custom-call(bf16[1,128,2048]{2,1,0:T(8,128)(2,1)} %grad.1, bf16[1,128,2048]{2,1,0:T(8,128)(2,1)} %sig.1, bf16[1,128,2048]{2,1,0:T(8,128)(2,1)} %gate.1, bf16[2048,128]{1,0:T(8,128)(2,1)} %taps.1, f32[16,128]{1,0:T(8,128)} %bitcast.1, ...), custom_call_target="tpu_custom_call" | custom-call | tf_op jit(solution)/shard_map/hyena_backward/pallas_call | solution.py:397
  71.2 0.0 copy-start
  71.2 1.9 %copy.20 = bf16[1,128,2048]{2,1,0:T(8,128)(2,1)} copy(bf16[1,128,2048]{2,1,0:T(8,128)(2,1)} %get-tuple-element.6) | data formatting | bytes 1048576
  73.2 0.0 copy-done
  73.2 0.0 copy-start.1
  73.2 0.8 %copy.21 = bf16[1,128,2048]{2,1,0:T(8,128)(2,1)} copy(bf16[1,128,2048]{2,1,0:T(8,128)(2,1)S(1)} %copy-done) | data formatting | bytes 1048576
  74.0 0.2 copy-done.1
  74.2 0.7 copy.22
Async XLA Ops:
  71.2 2.0 %copy-start = (bf16[1,128,2048]{2,1,0:T(8,128)(2,1)S(1)}, bf16[1,128,2048]{2,1,0:T(8,128)(2,1)}, u32[]{:S(2)}) copy-start(bf16[1,128,2048]{2,1,0:T(8,128)(2,1)} %get-tuple-element.7) | copy-start | bytes 1572868
  73.2 1.0 %copy-start.1 = (f32[64,512]{1,0:T(8,128)S(1)}, f32[64,512]{1,0:T(8,128)}, u32[]{:S(2)}) copy-start(f32[64,512]{1,0:T(8,128)} %get-tuple-element.8) | copy-start | bytes 393220

commit v4 on v3

--- a/solution.py
+++ b/solution.py
@@ -19,7 +19,6 @@
 GR = 8
 CI, CO = CC
 UN = 8
-UQ = 4
 
 
 def tables():
@@ -96,12 +95,6 @@
     docs_out[...] = docs_row
     docs_all[me] = docs_row
 
-    @pl.loop(0, 4)
-    def _(g):
-        for m in range(16):
-            cols = slice(128 * m, 128 * m + 128)
-            pair_store(sendu, g, m, sig[0, rows_of(g), cols].astype(F32), sig[0, rows_of(g + 4), cols].astype(F32))
-
     pl.semaphore_wait(barrier, NCTX - 1 + NX)
 
     @pl.loop(1, NCTX)
@@ -124,24 +117,31 @@
     own_taps = pltpu.make_async_copy(tap_rows(me), hall.at[xs, me], own.at[0])
     own_taps.start()
 
-    def spread(src, dst, chunk, chunks, sems, semr):
-        per = src.shape[0] // chunks
-        span = slice(per * chunk, per * chunk + per)
-
+    def send_part(src, dst, span, sems, semr):
         @pl.loop(1, NCTX)
         def _(p):
             peer = peer_of(p)
             pltpu.make_async_remote_copy(
-                src.at[span, peer], dst.at[span, me], sems.at[chunk], semr.at[chunk],
+                src.at[span, peer], dst.at[span, me], sems, semr,
                 device_id={"ctx": peer}, device_id_type=MESH,
             ).start()
+
+    def spread(src, dst, chunk, chunks, sems, semr):
+        per = src.shape[0] // chunks
+        send_part(src, dst, slice(per * chunk, per * chunk + per), sems.at[chunk], semr.at[chunk])
 
     def await_all(buf, chunk, chunks, sem):
         per = buf.shape[0] // chunks
         part = buf.at[per * chunk:per * chunk + per, 0:31]
         pltpu.make_async_copy(part, part, sem.at[chunk]).wait()
 
-    spread(sendu, recvu, 0, CI, u_s, u_r)
+    @pl.loop(0, 4)
+    def _(g):
+        for m in range(16):
+            cols = slice(128 * m, 128 * m + 128)
+            pair_store(sendu, g, m, sig[0, rows_of(g), cols].astype(F32), sig[0, rows_of(g + 4), cols].astype(F32))
+
+    send_part(sendu, recvu, slice(0, 1), u_s.at[0], u_r.at[0])
 
     own_taps.wait()
     pltpu.make_async_copy(hall.at[0, 0:31], hall.at[0, 0:31], tap_r).wait()
@@ -152,8 +152,7 @@
             hall.at[xs], hall.at[xs], gat_s, gat_r, device_id={"dp": x_of(q)}, device_id_type=MESH
         ).start()
 
-    for ch in range(1, CI):
-        spread(sendu, recvu, ch, CI, u_s, u_r)
+    send_part(sendu, recvu, slice(1, 4), u_s.at[1], u_r.at[1])
 
     def column(row):
         return jnp.broadcast_to(row.astype(F32), (128, 128)).T
@@ -203,7 +202,7 @@
     fone[...] = expand(first[...], 1024, 512)
     ftwo[...] = expand(last[...], 512, 1024)
 
-    @pl.loop(0, 32)
+    @pl.loop(0, 32, unroll=2)
     def _(k):
         ca, sa = cosa[pl.ds(k, 1), :], sina[pl.ds(k, 1), :]
         co = ca * cosb[...] - sa * sinb[...]
@@ -218,29 +217,25 @@
         matst[k, 128:256, 0:128] = sit.astype(BF)
         matst[k, 128:256, 128:256] = cot.astype(BF)
 
-    def stage_one(x, g):
+    def stage_one(x, g, lanes):
         y = jnp.dot(fone[...], x.reshape(512, 128), preferred_element_type=F32)
-        ybuf[:, :, g] = y.astype(BF).reshape(32, 2, 16, 128)
-        ybuf[:, :, g + 4] = swap(y).astype(BF).reshape(32, 2, 16, 128)
+        ybuf[:, :, g, :, 0:lanes] = y[:, 0:lanes].astype(BF).reshape(32, 2, 16, lanes)
+        ybuf[:, :, g + 4, :, 0:lanes] = swap(y)[:, 0:lanes].astype(BF).reshape(32, 2, 16, lanes)
 
     def stage_two(k):
         return jnp.dot(mats[k], ybuf[k].reshape(256, 128), preferred_element_type=F32)
 
     pltpu.make_async_copy(hall.at[0:3], hall.at[0:3], gat_r).wait()
 
-    @pl.loop(0, NCTX, unroll=2)
+    @pl.loop(0, NCTX, unroll=4)
     def _(a):
         block = hall[:, a].reshape(64, 128).astype(F32)
-        turned = jnp.concatenate([block, swap(block)], axis=0).T
+        turned = jnp.concatenate([swap(block), block], axis=0).T
         htime[:, a] = turned[0:64].astype(BF).reshape(4, 16, 128)
 
     @pl.loop(0, 4)
     def _(g):
-        stage_one(htime[g], g)
-
-    @pl.loop(0, 32, unroll=UQ)
-    def _(k):
-        hspec[k] = stage_two(k)
+        stage_one(htime[g], g, 128)
 
     gain = skip[pl.ds(me // 2, 1), :]
     turned_gain = pltpu.roll(jnp.broadcast_to(gain, (8, 128)), 64, axis=1)[0:1]
@@ -257,14 +252,15 @@
             both = jnp.where(half_low, v[c, 0], swap(v[c, 1]))
             buf[:, k, c] = both.astype(BF).reshape(4, 16, 128)
 
-    def bring(recv, local_copy, sem):
+    def bring(recv, local_copy, sem, spans):
         local_copy.wait()
-        for ch in range(CI):
-            await_all(recv, ch, CI, sem)
-
-            @pl.loop(4 // CI * ch, 4 // CI * ch + 4 // CI)
+        for ch, (start, stop) in enumerate(spans):
+            part = recv.at[start:stop, 0:31]
+            pltpu.make_async_copy(part, part, sem.at[ch]).wait()
+
+            @pl.loop(start, stop)
             def _(g):
-                stage_one(recv[g], g)
+                stage_one(recv[g], g, 64)
 
     def send_back(source, send, recv, chunks, sems, semr):
         for ch in chunks:
@@ -276,21 +272,23 @@
 
             spread(send, recv, ch, CO, sems, semr)
 
-    bring(recvu, own_u, u_r)
+    bring(recvu, own_u, u_r, ((0, 1), (1, 4)))
 
     @pl.loop(0, 32, unroll=UN)
     def _(k):
         s = stage_two(k)
         uspec[k] = s
+        h = swap(s)
+        hspec[k] = h
         sr, si = s[0:128], s[128:256]
-        hr, hi = hspec[k, 0:128], hspec[k, 128:256]
+        hr, hi = h[0:128], h[128:256]
         invert(k, jnp.concatenate([sr * hr - si * hi, sr * hi + si * hr], axis=0), vbuf)
 
     send_back(recvu, sendz, recvz, range(CO), z_s, z_r)
     own_z = pltpu.make_async_copy(sendz.at[:, me], recvz.at[:, me], own.at[2])
     own_z.start()
 
-    bring(recvd, own_d, d_r)
+    bring(recvd, own_d, d_r, ((0, 2), (2, 4)))
 
     @pl.loop(0, 32, unroll=UN)
     def _(k):
@@ -380,8 +378,10 @@
     pltpu.make_async_copy(docs_all.at[0:31], docs_all.at[0:31], doc_s).wait()
     pltpu.make_async_copy(hall.at[0, 0:31], hall.at[0, 0:31], tap_s).wait()
     pltpu.make_async_copy(hall.at[0:3], hall.at[0:3], gat_s).wait()
+    for ch, (start, stop) in enumerate(((0, 1), (1, 4))):
+        part = sendu.at[start:stop, 0:31]
+        pltpu.make_async_copy(part, part, u_s.at[ch]).wait()
     for ch in range(CI):
-        await_all(sendu, ch, CI, u_s)
         await_all(sendd, ch, CI, d_s)
     for ch in range(CO):
         await_all(sendz, ch, CO, z_s)

time: 75 us -> 73.8 us (0.984)
  Pallas kernels: 70.6 us -> 69.3 us
    pallas_call x1, Pallas kernels: 70.6 us -> 69.3 us  [local(): pl.pallas_call(kernel, out_shape=(token, token, jax.ShapeDtypeStruct((64,...]
where the time goes in v4:
time: 73.8 us; the launch traced here: 73.6 us
  Pallas kernels  69.3 us (94%)
  local copies, waits for them, and re-layouts  3.62 us (5%)
    pallas_call x1, Pallas kernels, local(): pl.pallas_call(kernel, out_shape=(token, token, jax.ShapeDtypeStruct((64,...  69.3 us
    unnamed x7, local copies, waits for them, and re-layouts  3.62 us

profile of v4, /device:TPU:1, one launch (start us, length us, event | category | flops | bytes accessed | tf_op | source)
XLA Modules:
  0.0 73.6 jit_solution(12299706556683537772)
XLA Ops:
  0.6 69.3 %hyena_backward.1 = (bf16[1,128,2048]{2,1,0:T(8,128)(2,1)}, bf16[1,128,2048]{2,1,0:T(8,128)(2,1)}, f32[64,512]{1,0:T(8,128)}) custom-call(bf16[1,128,2048]{2,1,0:T(8,128)(2,1)} %grad.1, bf16[1,128,2048]{2,1,0:T(8,128)(2,1)} %sig.1, bf16[1,128,2048]{2,1,0:T(8,128)(2,1)} %gate.1, bf16[2048,128]{1,0:T(8,128)(2,1)} %taps.1, f32[16,128]{1,0:T(8,128)} %bitcast.1, ...), custom_call_target="tpu_custom_call" | custom-call | tf_op jit(solution)/shard_map/hyena_backward/pallas_call | solution.py:397
  70.0 0.0 copy-start
  70.0 1.9 %copy.20 = bf16[1,128,2048]{2,1,0:T(8,128)(2,1)} copy(bf16[1,128,2048]{2,1,0:T(8,128)(2,1)} %get-tuple-element.6) | data formatting | bytes 1048576
  71.9 0.0 copy-done
  71.9 0.0 copy-start.1
  71.9 0.8 %copy.21 = bf16[1,128,2048]{2,1,0:T(8,128)(2,1)} copy(bf16[1,128,2048]{2,1,0:T(8,128)(2,1)S(1)} %copy-done) | data formatting | bytes 1048576
  72.7 0.2 copy-done.1
  72.9 0.7 copy.22
Async XLA Ops:
  70.0 2.0 %copy-start = (bf16[1,128,2048]{2,1,0:T(8,128)(2,1)S(1)}, bf16[1,128,2048]{2,1,0:T(8,128)(2,1)}, u32[]{:S(2)}) copy-start(bf16[1,128,2048]{2,1,0:T(8,128)(2,1)} %get-tuple-element.7) | copy-start | bytes 1572868
  71.9 1.0 %copy-start.1 = (f32[64,512]{1,0:T(8,128)S(1)}, f32[64,512]{1,0:T(8,128)}, u32[]{:S(2)}) copy-start(f32[64,512]{1,0:T(8,128)} %get-tuple-element.8) | copy-start | bytes 393220

commit v5 on v4

--- a/solution.py
+++ b/solution.py
@@ -19,6 +19,7 @@
 GR = 8
 CI, CO = CC
 UN = 8
+US = 31
 
 
 def tables():
@@ -52,9 +53,9 @@
 
 
 def kernel(
-    grad, sig, gate, taps, skip, lang, docs, dro, first, last, cosa, sina, cosb, sinb,
+    grad_hbm, sig_hbm, gate_hbm, taps, skip, lang, docs, dro, first, last, cosa, sina, cosb, sinb,
     d_input, d_gate, d_filter,
-    docs_out, docs_all, hall, htime, scale, mats, matst, fone, ftwo, sendu, recvu, sendd, recvd, sendz, recvz,
+    grad, sig, gate, stage, docs_out, docs_all, hall, htime, scale, mats, matst, fone, ftwo, sendu, recvu, sendd, recvd, sendz, recvz,
     sendi, recvi, ybuf, vbuf, qbuf, hspec, uspec, gspec, dfs, dfr, dft, dfq,
     doc_s, doc_r, tap_s, tap_r, gat_s, gat_r, u_s, u_r, d_s, d_r, z_s, z_r, i_s, i_r, df_s, df_r, dq_s, dq_r, own,
 ):
@@ -70,6 +71,12 @@
     def x_of(q):
         return zl * NX + lax.rem(xs + q, NX)
 
+    staged = [
+        pltpu.make_async_copy(src, dst, stage.at[i])
+        for i, (src, dst) in enumerate(((sig_hbm, sig), (grad_hbm, grad), (gate_hbm, gate)))
+    ]
+    for copy in staged:
+        copy.start()
     barrier = pltpu.get_barrier_semaphore()
 
     @pl.loop(1, NCTX)
@@ -118,7 +125,7 @@
     own_taps.start()
 
     def send_part(src, dst, span, sems, semr):
-        @pl.loop(1, NCTX)
+        @pl.loop(1, NCTX, unroll=US)
         def _(p):
             peer = peer_of(p)
             pltpu.make_async_remote_copy(
@@ -135,6 +142,8 @@
         part = buf.at[per * chunk:per * chunk + per, 0:31]
         pltpu.make_async_copy(part, part, sem.at[chunk]).wait()
 
+    staged[0].wait()
+
     @pl.loop(0, 4)
     def _(g):
         for m in range(16):
@@ -153,6 +162,9 @@
         ).start()
 
     send_part(sendu, recvu, slice(1, 4), u_s.at[1], u_r.at[1])
+
+    staged[1].wait()
+    staged[2].wait()
 
     def column(row):
         return jnp.broadcast_to(row.astype(F32), (128, 128)).T
@@ -397,9 +409,11 @@
     return pl.pallas_call(
         kernel,
         out_shape=(token, token, jax.ShapeDtypeStruct((64, 512), F32)),
-        in_specs=[vmem] * 7 + [pl.BlockSpec(memory_space=pltpu.SMEM)] + [vmem] * 6,
+        in_specs=[pl.BlockSpec(memory_space=pl.ANY)] * 4 + [vmem] * 3 + [pl.BlockSpec(memory_space=pltpu.SMEM)] + [vmem] * 6,
         out_specs=(vmem, vmem, vmem),
         scratch_shapes=[
+            *[pltpu.VMEM((1, 128, 2048), BF)] * 3,
+            dma((3,)),
             pltpu.VMEM((1, 128), jnp.int32),
             pltpu.VMEM((NCTX, 1, 128), jnp.int32),
             pltpu.VMEM((NX, NCTX, 16, 128), BF),
@@ -426,7 +440,7 @@
             dma, dma, dma, dma, dma((5,)),
         ],
         compiler_params=pltpu.CompilerParams(
-            collective_id=0, has_side_effects=True, vmem_limit_bytes=56 << 20
+            collective_id=0, has_side_effects=True, vmem_limit_bytes=60 << 20
         ),
         name="hyena_backward",
     )(

time: 73.8 us -> 73.3 us (level)
  no operation moved by 1% of the time
where the time goes in v5:
time: 73.3 us; the launch traced here: 73.1 us
  Pallas kernels  68.8 us (94%)
  local copies, waits for them, and re-layouts  3.62 us (5%)
    pallas_call x1, Pallas kernels, local(): pl.pallas_call(kernel, out_shape=(token, token, jax.ShapeDtypeStruct((64,...  68.8 us
    unnamed x7, local copies, waits for them, and re-layouts  3.62 us

profile of v5, /device:TPU:1, one launch (start us, length us, event | category | flops | bytes accessed | tf_op | source)
XLA Modules:
  0.0 73.1 jit_solution(3021310992239533632)
XLA Ops:
  0.6 68.8 %hyena_backward.1 = (bf16[1,128,2048]{2,1,0:T(8,128)(2,1)}, bf16[1,128,2048]{2,1,0:T(8,128)(2,1)}, f32[64,512]{1,0:T(8,128)}) custom-call(bf16[1,128,2048]{2,1,0:T(8,128)(2,1)} %grad_hbm.1, bf16[1,128,2048]{2,1,0:T(8,128)(2,1)} %sig_hbm.1, bf16[1,128,2048]{2,1,0:T(8,128)(2,1)} %gate_hbm.1, bf16[2048,128]{1,0:T(8,128)(2,1)} %taps.1, f32[16,128]{1,0:T(8,128)} %bitcast.1, ...), custom_call_target="tpu_custom_call" | custom-call | tf_op jit(solution)/shard_map/hyena_backward/pallas_call | solution.py:409
  69.5 0.0 copy-start
  69.5 1.9 %copy.20 = bf16[1,128,2048]{2,1,0:T(8,128)(2,1)} copy(bf16[1,128,2048]{2,1,0:T(8,128)(2,1)} %get-tuple-element.6) | data formatting | bytes 1048576
  71.4 0.0 copy-done
  71.4 0.0 copy-start.1
  71.4 0.8 %copy.21 = bf16[1,128,2048]{2,1,0:T(8,128)(2,1)} copy(bf16[1,128,2048]{2,1,0:T(8,128)(2,1)S(1)} %copy-done) | data formatting | bytes 1048576
  72.2 0.2 copy-done.1
  72.5 0.7 copy.22
Async XLA Ops:
  69.5 2.0 %copy-start = (bf16[1,128,2048]{2,1,0:T(8,128)(2,1)S(1)}, bf16[1,128,2048]{2,1,0:T(8,128)(2,1)}, u32[]{:S(2)}) copy-start(bf16[1,128,2048]{2,1,0:T(8,128)(2,1)} %get-tuple-element.7) | copy-start | bytes 1572868
  71.4 1.0 %copy-start.1 = (f32[64,512]{1,0:T(8,128)S(1)}, f32[64,512]{1,0:T(8,128)}, u32[]{:S(2)}) copy-start(f32[64,512]{1,0:T(8,128)} %get-tuple-element.8) | copy-start | bytes 393220

commit v6 on v5

--- a/solution.py
+++ b/solution.py
@@ -20,6 +20,7 @@
 CI, CO = CC
 UN = 8
 US = 31
+BACK = ((0, 1), (1, 4))
 
 
 def tables():
@@ -276,13 +277,15 @@
 
     def send_back(source, send, recv, chunks, sems, semr):
         for ch in chunks:
-            @pl.loop(4 // CO * ch, 4 // CO * ch + 4 // CO)
+            start, stop = BACK[ch]
+
+            @pl.loop(start, stop)
             def _(g):
                 o = jnp.dot(ftwo[...], vbuf[g].reshape(1024, 128), preferred_element_type=F32)
                 o = o + gain2 * source[g].reshape(512, 128).astype(F32)
                 send[g] = o.astype(BF).reshape(32, 16, 128)
 
-            spread(send, recv, ch, CO, sems, semr)
+            send_part(send, recv, slice(start, stop), sems.at[ch], semr.at[ch])
 
     bring(recvu, own_u, u_r, ((0, 1), (1, 4)))
 
@@ -359,10 +362,15 @@
         left, right = recv[g, 2 * m].astype(F32), recv[g, 2 * m + 1].astype(F32)
         return jnp.where(low, left, swap(right)), jnp.where(low, swap(left), right)
 
+    def await_span(buf, ch, sem):
+        start, stop = BACK[ch]
+        part = buf.at[start:stop, 0:31]
+        pltpu.make_async_copy(part, part, sem.at[ch]).wait()
+
     for ch in range(CO):
-        await_all(recvz, ch, CO, z_r)
-
-        @pl.loop(4 // CO * ch, 4 // CO * ch + 4 // CO)
+        await_span(recvz, ch, z_r)
+
+        @pl.loop(*BACK[ch])
         def _(g):
             for m in range(16):
                 cols = slice(128 * m, 128 * m + 128)
@@ -371,9 +379,9 @@
                     d_gate[0, rows, cols] = (grad[0, rows, cols].astype(F32) * scale[rows, :] * z).astype(BF)
 
     for ch in range(CO):
-        await_all(recvi, ch, CO, i_r)
-
-        @pl.loop(4 // CO * ch, 4 // CO * ch + 4 // CO)
+        await_span(recvi, ch, i_r)
+
+        @pl.loop(*BACK[ch])
         def _(g):
             for m in range(16):
                 cols = slice(128 * m, 128 * m + 128)
@@ -396,8 +404,8 @@
     for ch in range(CI):
         await_all(sendd, ch, CI, d_s)
     for ch in range(CO):
-        await_all(sendz, ch, CO, z_s)
-        await_all(sendi, ch, CO, i_s)
+        await_span(sendz, ch, z_s)
+        await_span(sendi, ch, i_s)
     pltpu.make_async_copy(dfs.at[0:3], dfs.at[0:3], df_s).wait()
     swap_df.wait_send()
 

time: 73.3 us -> 73.1 us (level)
  no operation moved by 1% of the time
where the time goes in v6:
time: 73.1 us; the launch traced here: 72.9 us
  Pallas kernels  68.6 us (94%)
  local copies, waits for them, and re-layouts  3.62 us (5%)
    pallas_call x1, Pallas kernels, local(): pl.pallas_call(kernel, out_shape=(token, token, jax.ShapeDtypeStruct((64,...  68.6 us
    unnamed x7, local copies, waits for them, and re-layouts  3.62 us

profile of v6, /device:TPU:1, one launch (start us, length us, event | category | flops | bytes accessed | tf_op | source)
XLA Modules:
  0.0 72.9 jit_solution(2994362337472331055)
XLA Ops:
  0.6 68.6 %hyena_backward.1 = (bf16[1,128,2048]{2,1,0:T(8,128)(2,1)}, bf16[1,128,2048]{2,1,0:T(8,128)(2,1)}, f32[64,512]{1,0:T(8,128)}) custom-call(bf16[1,128,2048]{2,1,0:T(8,128)(2,1)} %grad_hbm.1, bf16[1,128,2048]{2,1,0:T(8,128)(2,1)} %sig_hbm.1, bf16[1,128,2048]{2,1,0:T(8,128)(2,1)} %gate_hbm.1, bf16[2048,128]{1,0:T(8,128)(2,1)} %taps.1, f32[16,128]{1,0:T(8,128)} %bitcast.1, ...), custom_call_target="tpu_custom_call" | custom-call | tf_op jit(solution)/shard_map/hyena_backward/pallas_call | solution.py:417
  69.3 0.0 copy-start
  69.3 1.9 %copy.20 = bf16[1,128,2048]{2,1,0:T(8,128)(2,1)} copy(bf16[1,128,2048]{2,1,0:T(8,128)(2,1)} %get-tuple-element.6) | data formatting | bytes 1048576
  71.2 0.0 copy-done
  71.2 0.0 copy-start.1
  71.2 0.8 %copy.21 = bf16[1,128,2048]{2,1,0:T(8,128)(2,1)} copy(bf16[1,128,2048]{2,1,0:T(8,128)(2,1)S(1)} %copy-done) | data formatting | bytes 1048576
  72.0 0.2 copy-done.1
  72.3 0.7 copy.22
Async XLA Ops:
  69.3 2.0 %copy-start = (bf16[1,128,2048]{2,1,0:T(8,128)(2,1)S(1)}, bf16[1,128,2048]{2,1,0:T(8,128)(2,1)}, u32[]{:S(2)}) copy-start(bf16[1,128,2048]{2,1,0:T(8,128)(2,1)} %get-tuple-element.7) | copy-start | bytes 1572868
  71.2 1.0 %copy-start.1 = (f32[64,512]{1,0:T(8,128)S(1)}, f32[64,512]{1,0:T(8,128)}, u32[]{:S(2)}) copy-start(f32[64,512]{1,0:T(8,128)} %get-tuple-element.8) | copy-start | bytes 393220
